TPU v7x, 32 devices: a whole 2x2x4 slice. The times are simulated.
32 devices in a mesh: grp: 2 (over x), px: 4 (over y, core), py: 4 (over z).
Axes of the slice: x: 2, y: 2, z: 4, core: 2. Of those that a mesh axis runs over, the one named last changes fastest.
Arguments:
- multiplier: float32 [3, 32, 16, 256, 256], P(None, 'py', None, ('grp', 'px')), may hold values from -6 to 6
- auxiliary: float32 [3, 32, 16, 256, 256], P(None, 'py', None, ('grp', 'px')), may hold values from -6 to 6
- density_start: float32 [16, 256, 256], P(None, ('grp', 'px')), may hold values from 0.5 to 2
- density_end: float32 [16, 256, 256], P(None, ('grp', 'px')), may hold values from 0.5 to 2
Outputs:
- multiplier_next: float32 [3, 32, 16, 256, 256], P(None, 'py', None, ('grp', 'px'))
- auxiliary_next: float32 [3, 32, 16, 256, 256], P(None, 'py', None, ('grp', 'px'))
All inputs are finite; a program needn't handle non-finite values.
Results may differ from a plain program's by a relative error of at most 0.0003.
Values sent between devices are 32-bit elements; how exact they have to be, the bound alone decides.
A program may use at most 128 MiB of HBM per device.

v0:
```python
import functools
import math

import jax
import jax.numpy as jnp
from jax import lax
from jax.experimental import pallas as pl
from jax.experimental.pallas import tpu as pltpu
from jax.sharding import PartitionSpec as P

NEWTON = 4
PENALTY = 1.0
PRECISE = lax.Precision.HIGHEST
VMEM_LIMIT = 60 * 1024 * 1024
SPACE = ("grp", "px")


def dot(a, b):
    return jnp.dot(a, b, precision=PRECISE, preferred_element_type=jnp.float32)


def hartley_table(length):
    row_index = lax.broadcasted_iota(jnp.int32, (length, length), 0)
    col_index = lax.broadcasted_iota(jnp.int32, (length, length), 1)
    phase_index = row_index * col_index % length
    angles = phase_index.astype(jnp.float32) * (2.0 * math.pi / length)
    return (jnp.cos(angles) + jnp.sin(angles)) / math.sqrt(length)


def mode_tables(rows, cols, here, blocks, block):
    m = lax.broadcasted_iota(jnp.int32, (rows, cols), 0)
    n = lax.broadcasted_iota(jnp.int32, (rows, cols), 1)
    m = jnp.minimum(m, rows - m).astype(jnp.float32)
    n = jnp.minimum(n, cols - n).astype(jnp.float32)
    lam = 4.0 * jnp.sin(m * (math.pi / rows)) ** 2 + 4.0 * jnp.sin(n * (math.pi / cols)) ** 2
    sinh = jnp.sqrt(lam * (1.0 + 0.25 * lam))
    inverse = 1.0 + 0.5 * lam + sinh
    ratio = 1.0 / inverse
    step = lax.integer_pow(ratio, here)
    double = step * step
    low = jnp.ones_like(step)
    high = jnp.ones_like(step)
    full = double
    for k in range(1, blocks):
        low = jnp.where(block >= k, low * double, low)
        high = jnp.where(blocks - 1 - block >= k, high * double, high)
        full = full * double
    positive = lam > 0.0
    scale = jnp.where(
        positive, 0.5 / jnp.where(positive, sinh * (1.0 - full), 1.0), 0.0
    )
    return jnp.stack([ratio, inverse, low, high, scale]), step


def source_kernel(mult, aux, start, end, table, out, prev, body, tail, *, levels):
    t = pl.program_id(0)
    here = pl.num_programs(0)
    problems, rows, cols = body.shape
    group, per = out.shape[0], out.shape[1]
    level = lax.axis_index("py") * here + t
    first = level == 0
    last = level == levels - 1

    @pl.when(t == 0)
    def _():
        prev[...] = jnp.zeros_like(prev)
        tail[...] = jnp.zeros_like(tail)

    row = lax.broadcasted_iota(jnp.int32, (rows, cols), 0)
    keep = jnp.where(last, 0.0, 1.0)
    begin = jnp.where(first, -1.0 / PENALTY, 0.0)
    finish = jnp.where(last, 1.0 / PENALTY, 0.0)

    def one(b, carry):
        along = aux[1, 0, b] - mult[1, 0, b] / PENALTY
        beside = jnp.where(row == 0, 0.0, pltpu.roll(along, 1, 0))
        second = aux[2, 0, b] - mult[2, 0, b] / PENALTY
        across = pltpu.roll(second, 1, 1) - second
        now = (aux[0, 0, b] - mult[0, 0, b] / PENALTY) * keep
        boundary = begin * start[b] + finish * end[b]
        body[b] = prev[b] - now + beside - along + across + boundary
        prev[b] = now
        tail[b, pl.ds(t, 1), :] = along[rows - 1 :, :]
        return carry

    lax.fori_loop(0, problems, one, 0, unroll=4)
    spread = dot(body[...].reshape(problems * rows, cols), table[...])
    at = pl.multiple_of(t * rows, rows)
    out[:, :, pl.ds(at, rows), :] = spread.reshape(group, per, rows, cols)

    @pl.when(t == here - 1)
    def _():
        beyond = dot(prev[...].reshape(problems * rows, cols), table[...])
        out[:, :, here * rows : here * rows + rows, :] = beyond.reshape(group, per, rows, cols)
        held = tail.shape[1]
        rims = dot(tail[...].reshape(problems * held, cols), table[...])
        out[:, :, here * rows + rows :, :] = rims.reshape(group, per, held, cols)


def forward_kernel(x, table, coef, modes, up, down, plane, *, here, rows):
    group = x.shape[0]
    total, cols = table.shape[0], x.shape[3]

    def one(t, carry):
        at = pl.multiple_of(t * rows, rows)
        plane[...] = x[:, 0, pl.ds(at, rows), :].reshape(total, cols)

        @pl.when(t < here)
        def _():
            for q in range(group):
                to = rows * ((q + 1) % group)
                plane[to : to + 1, :] += x[q, 0, pl.ds(here * rows + rows + t, 1), :]

        modes[0, t] = dot(table[...], plane[...])
        return carry

    lax.fori_loop(0, here + 1, one, 0)

    def sweep(c, carry):
        cut = pl.ds(pl.multiple_of(c * 8, 8), 8)
        ratio, inverse, low, high = (coef[k, cut, :] for k in range(4))
        square = ratio * ratio
        power = low * ratio
        total_up = jnp.zeros_like(ratio)
        for level in range(here + 1):
            total_up = ratio * total_up + (1.0 + power) * modes[0, level, cut, :]
            power = power * square
        up[0, cut, :] = total_up
        power = high * inverse
        total_down = jnp.zeros_like(ratio)
        for level in range(here, -1, -1):
            total_down = ratio * total_down + (1.0 + power) * modes[0, level, cut, :]
            power = power * square
        down[0, cut, :] = total_down
        return carry

    lax.fori_loop(0, total // 8, sweep, 0, unroll=4)


def carry_kernel(up_own, down_own, step, up_in, down_in, up_got, down_got, up_out, down_out,
                 up_sent, up_came, down_sent, down_came, *, blocks, pieces, lag):
    me = lax.axis_index("py")
    size = up_own.shape[1] // pieces
    has_lower = me > 0
    has_upper = me < blocks - 1
    pairs = [(b, c) for b in range(up_own.shape[0]) for c in range(pieces)]

    def copy(source, target, sent, came, k, other):
        b, c = pairs[k]
        cut = pl.ds(c * size, size)
        return pltpu.make_async_remote_copy(
            src_ref=source.at[b, cut, :],
            dst_ref=target.at[b, cut, :],
            send_sem=sent.at[k],
            recv_sem=came.at[k],
            device_id={"py": other},
            device_id_type=pl.DeviceIdType.MESH,
        )

    barrier = pltpu.get_barrier_semaphore()

    @pl.when(has_lower)
    def _():
        pl.semaphore_signal(
            barrier, inc=1, device_id={"py": me - 1}, device_id_type=pl.DeviceIdType.MESH
        )

    @pl.when(has_upper)
    def _():
        pl.semaphore_signal(
            barrier, inc=1, device_id={"py": me + 1}, device_id_type=pl.DeviceIdType.MESH
        )

    @pl.when(has_lower & has_upper)
    def _():
        pl.semaphore_wait(barrier, 2)

    @pl.when(jnp.logical_not(has_lower & has_upper))
    def _():
        pl.semaphore_wait(barrier, 1)

    def relay(k, own, got, out, sent, came, first, last, ahead):
        b, c = pairs[k]
        cut = pl.ds(c * size, size)

        @pl.when(jnp.logical_not(first))
        def _():
            copy(out, got, sent, came, k, ahead).wait_recv()

            @pl.when(jnp.logical_not(last))
            def _():
                out[b, cut, :] = own[b, cut, :] + step[cut, :] * got[b, cut, :]
                copy(out, got, sent, came, k, ahead).start()

    up = (up_own, up_got, up_out, up_sent, up_came, me == 0, me == blocks - 1,
          (me + 1) % blocks)
    down = (down_own, down_got, down_out, down_sent, down_came, me == blocks - 1, me == 0,
            (me + blocks - 1) % blocks)

    @pl.when(me == 0)
    def _():
        for k in range(len(pairs)):
            copy(up_own, up_got, up_sent, up_came, k, me + 1).start()

    @pl.when(me == blocks - 1)
    def _():
        for k in range(len(pairs)):
            copy(down_own, down_got, down_sent, down_came, k, me - 1).start()

    def weave(early, late):
        for k in range(len(pairs) + lag):
            if k < len(pairs):
                relay(k, *early)
            if k >= lag:
                relay(k - lag, *late)

    lower_half = me < blocks // 2

    @pl.when(lower_half)
    def _():
        weave(up, down)

    @pl.when(jnp.logical_not(lower_half))
    def _():
        weave(down, up)

    @pl.when(has_lower)
    def _():
        up_in[...] = up_got[...]
        for k in range(len(pairs)):
            copy(down_out, down_got, down_sent, down_came, k, me - 1).wait_send()

    @pl.when(me == 0)
    def _():
        up_in[...] = jnp.zeros_like(up_in)

    @pl.when(has_upper)
    def _():
        down_in[...] = down_got[...]
        for k in range(len(pairs)):
            copy(up_out, up_got, up_sent, up_came, k, me + 1).wait_send()

    @pl.when(me == blocks - 1)
    def _():
        down_in[...] = jnp.zeros_like(down_in)


def backward_kernel(modes, up, down, table, coef, out, phi, *, here, rows, levels):
    group = out.shape[0]
    total, cols = table.shape[0], out.shape[3]

    def sweep(c, carry):
        cut = pl.ds(pl.multiple_of(c * 8, 8), 8)
        ratio, inverse, low, high, scale = (coef[k, cut, :] for k in range(5))
        square = ratio * ratio
        powers_low = []
        powers_high = []
        power = low * ratio
        for level in range(here + 1):
            powers_low.append(1.0 + power)
            power = power * square
        power = high * inverse
        for level in range(here + 1):
            powers_high.append(1.0 + power)
            power = power * square
        powers_high = powers_high[::-1]
        value = up[0, cut, :]
        for level in range(here + 1):
            if level:
                value = ratio * value
            value = value + powers_low[level] * modes[0, level, cut, :]
            phi[level, cut, :] = powers_high[level] * value
        behind = down[0, cut, :]
        for level in range(here, -1, -1):
            phi[level, cut, :] = scale * (phi[level, cut, :] + powers_low[level] * behind)
            behind = ratio * (behind + powers_high[level] * modes[0, level, cut, :])
        return carry

    lax.fori_loop(0, total // 8, sweep, 0, unroll=4)

    first = lax.axis_index("py") * here
    tile = (slice(0, 8), slice(0, 128))
    flat = (lax.broadcasted_iota(jnp.int32, (8, 128), 0) == 0) & (
        lax.broadcasted_iota(jnp.int32, (8, 128), 1) == 0
    )
    below = 0.5 * up[0, 0:8, 0:128]
    whole = below + 0.5 * down[0, 0:8, 0:128]
    for level in range(here + 1):
        whole = whole + modes[0, level, 0:8, 0:128]
    mean = whole * (1.0 / levels)
    value = jnp.zeros((8, 128), jnp.float32)
    for level in range(here + 1):
        phi[level, 0:8, 0:128] = jnp.where(flat, value, phi[level, 0:8, 0:128])
        if level < here:
            below = below + modes[0, level, 0:8, 0:128]
            count = (first + (level + 1)).astype(jnp.float32)
            value = value - (below - count * mean)

    if out.shape[2] > here * rows + rows + here:
        out[:, :, here * rows + rows :, :] = jnp.zeros(
            (group, 1, out.shape[2] - here * rows - rows, cols), jnp.float32
        )

    def one(t, carry):
        at = pl.multiple_of(t * rows, rows)
        field = dot(table[...], phi[t])
        out[:, 0, pl.ds(at, rows), :] = field.reshape(group, rows, cols)

        @pl.when(t < here)
        def _():
            for d in range(group):
                take = rows * ((d + 1) % group)
                out[d, 0, pl.ds(here * rows + rows + t, 1), :] = field[take : take + 1, :]

        return carry

    lax.fori_loop(0, here + 1, one, 0)


def project_kernel(
    x, mult, table, next_mult, next_aux, phi, following, rims, *, levels
):
    t = pl.program_id(0)
    here = pl.num_programs(0)
    problems, rows, cols = phi.shape
    held = rims.shape[1]
    level = lax.axis_index("py") * here + t
    moving = jnp.where(level == levels - 1, 0.0, 1.0)

    def field(at):
        flat = x[:, :, pl.ds(at, rows), :].reshape(problems * rows, cols)
        return dot(flat, table[...]).reshape(problems, rows, cols)

    @pl.when(t == 0)
    def _():
        following[...] = field(0)
        edge = x[:, :, here * rows + rows :, :].reshape(problems * held, cols)
        rims[...] = dot(edge, table[...]).reshape(problems, held, cols)

    phi[...] = following[...]
    following[...] = field(pl.multiple_of((t + 1) * rows, rows))
    row = lax.broadcasted_iota(jnp.int32, (rows, cols), 0)

    def one(b, carry):
        here_phi = phi[b]
        rim = jnp.broadcast_to(rims[b, pl.ds(t, 1), :], (rows, cols))
        grad_time = (following[b] - here_phi) * moving
        grad_first = jnp.where(row == rows - 1, rim, pltpu.roll(here_phi, rows - 1, 0)) - here_phi
        grad_second = pltpu.roll(here_phi, cols - 1, 1) - here_phi
        mult_time, mult_first, mult_second = (mult[k, 0, b] for k in range(3))
        time_part = grad_time + mult_time / PENALTY
        first = grad_first + mult_first / PENALTY
        second = grad_second + mult_second / PENALTY
        kinetic = 0.5 * (first * first + second * second)
        offset_one = 1.0 + time_part
        solid = kinetic > 1e-37
        root = jnp.exp(jnp.log(jnp.where(solid, kinetic, 1.0)) * (1.0 / 3.0))
        scaling = jnp.maximum(offset_one, 1.0) + jnp.where(solid, root, 0.0)
        for newton_step in range(NEWTON):
            residue = scaling * scaling * (scaling - offset_one) - kinetic
            derivative = scaling * (3.0 * scaling - 2.0 * offset_one)
            scaling = jnp.maximum(scaling - residue / derivative, 1.0)
        feasible = time_part + kinetic <= 0.0
        shrink = jnp.where(feasible, 1.0, 1.0 / scaling)
        out_time = jnp.where(feasible, time_part, time_part - (scaling - 1.0))
        out_first = first * shrink
        out_second = second * shrink
        next_aux[0, 0, b] = out_time
        next_aux[1, 0, b] = out_first
        next_aux[2, 0, b] = out_second
        next_mult[0, 0, b] = mult_time + PENALTY * (grad_time - out_time)
        next_mult[1, 0, b] = mult_first + PENALTY * (grad_first - out_first)
        next_mult[2, 0, b] = mult_second + PENALTY * (grad_second - out_second)
        return carry

    lax.fori_loop(0, problems, one, 0, unroll=2)


def params():
    return pltpu.CompilerParams(vmem_limit_bytes=VMEM_LIMIT)


def whole_block(shape):
    return pl.BlockSpec(shape, lambda *_: (0,) * len(shape))


def local(multiplier, auxiliary, density_start, density_end):
    _, here, problems, rows, cols = multiplier.shape
    blocks = lax.axis_size("py")
    levels = here * blocks
    group = lax.axis_size("grp") * lax.axis_size("px")
    per = problems // group
    row_total = rows * group
    held = -(-here // 8) * 8
    packed = here * rows + rows + held
    f32 = jnp.float32
    table_cols = hartley_table(cols)
    table_rows = hartley_table(row_total)
    coef, step = mode_tables(row_total, cols, here, blocks, lax.axis_index("py"))

    level_block = pl.BlockSpec((3, 1, problems, rows, cols), lambda t: (0, t, 0, 0, 0))
    density_block = whole_block((problems, rows, cols))
    payload = pl.pallas_call(
        functools.partial(source_kernel, levels=levels),
        out_shape=jax.ShapeDtypeStruct((group, per, packed, cols), f32),
        grid=(here,),
        in_specs=[level_block, level_block, density_block, density_block, whole_block((cols, cols))],
        out_specs=whole_block((group, per, packed, cols)),
        scratch_shapes=[
            pltpu.VMEM((problems, rows, cols), f32),
            pltpu.VMEM((problems, rows, cols), f32),
            pltpu.VMEM((problems, held, cols), f32),
        ],
        compiler_params=params(),
        name="source",
    )(multiplier, auxiliary, density_start, density_end, table_cols)

    pencil = lax.all_to_all(payload, SPACE, split_axis=0, concat_axis=0, tiled=True)

    pencil_block = pl.BlockSpec((group, 1, packed, cols), lambda b: (0, b, 0, 0))
    modes_block = pl.BlockSpec((1, here + 1, row_total, cols), lambda b: (b, 0, 0, 0))
    carry_block = pl.BlockSpec((1, row_total, cols), lambda b: (b, 0, 0))
    carry_shape = jax.ShapeDtypeStruct((per, row_total, cols), f32)
    modes, up_own, down_own = pl.pallas_call(
        functools.partial(forward_kernel, here=here, rows=rows),
        out_shape=(
            jax.ShapeDtypeStruct((per, here + 1, row_total, cols), f32),
            carry_shape,
            carry_shape,
        ),
        grid=(per,),
        in_specs=[pencil_block, whole_block((row_total, row_total)), whole_block(coef.shape)],
        out_specs=(modes_block, carry_block, carry_block),
        scratch_shapes=[pltpu.VMEM((row_total, cols), f32)],
        compiler_params=params(),
        name="forward",
    )(pencil, table_rows, coef)

    pieces = math.gcd(row_total // 8, 4)
    count = per * pieces
    vmem = pl.BlockSpec(memory_space=pltpu.VMEM)
    up_in, down_in = pl.pallas_call(
        functools.partial(carry_kernel, blocks=blocks, pieces=pieces, lag=min(3, count)),
        out_shape=(carry_shape, carry_shape),
        in_specs=[vmem, vmem, vmem],
        out_specs=(vmem, vmem),
        scratch_shapes=[pltpu.VMEM((per, row_total, cols), f32)] * 4
        + [pltpu.SemaphoreType.DMA((count,))] * 4,
        compiler_params=pltpu.CompilerParams(
            collective_id=0, has_side_effects=True, vmem_limit_bytes=24 * 1024 * 1024
        ),
        name="carry",
    )(up_own, down_own, step)

    returned = pl.pallas_call(
        functools.partial(backward_kernel, here=here, rows=rows, levels=levels),
        out_shape=jax.ShapeDtypeStruct((group, per, packed, cols), f32),
        grid=(per,),
        in_specs=[
            modes_block,
            carry_block,
            carry_block,
            whole_block((row_total, row_total)),
            whole_block(coef.shape),
        ],
        out_specs=pencil_block,
        scratch_shapes=[pltpu.VMEM((here + 1, row_total, cols), f32)],
        compiler_params=params(),
        name="backward",
    )(modes, up_in, down_in, table_rows, coef)

    slab = lax.all_to_all(returned, SPACE, split_axis=0, concat_axis=0, tiled=True)

    out_shape = jax.ShapeDtypeStruct(multiplier.shape, f32)
    return pl.pallas_call(
        functools.partial(project_kernel, levels=levels),
        out_shape=(out_shape, out_shape),
        grid=(here,),
        in_specs=[
            whole_block((group, per, packed, cols)),
            level_block,
            whole_block((cols, cols)),
        ],
        out_specs=(level_block, level_block),
        scratch_shapes=[
            pltpu.VMEM((problems, rows, cols), f32),
            pltpu.VMEM((problems, rows, cols), f32),
            pltpu.VMEM((problems, held, cols), f32),
        ],
        compiler_params=params(),
        name="project",
    )(slab, multiplier, table_cols)


def solution(mesh):
    placed = (
        P(None, "py", None, ("grp", "px"), None),
        P(None, "py", None, ("grp", "px"), None),
        P(None, ("grp", "px"), None),
        P(None, ("grp", "px"), None),
    )
    return jax.shard_map(
        local,
        mesh=mesh,
        in_specs=placed,
        out_specs=(
            P(None, "py", None, ("grp", "px"), None),
            P(None, "py", None, ("grp", "px"), None),
        ),
        check_vma=False,
    )
```

profile of v0, /device:TPU:0, one launch (start us, length us, event | category | flops | bytes accessed | tf_op | source)
XLA Modules:
  0.0 221.5 jit_solution(193117878930493200)
XLA Ops:
  0.6 1.7 add_multiply_fusion.4.table
  2.4 16.6 %source.1 = f32[8,2,296,256]{3,2,1,0:T(8,128)} custom-call(f32[3,8,16,32,256]{4,3,2,1,0:T(8,128)} %mult.3, f32[3,8,16,32,256]{4,3,2,1,0:T(8,128)} %aux.1, f32[16,32,256]{2,1,0:T(8,128)} %start.1, f32[16,32,256]{2,1,0:T(8,128)} %end.1, f32[256,256]{1,0:T(8,128)} %add_multiply_fusion.4.table), custom_call_target="tpu_custom_call" | custom-call | tf_op jit(solution)/shard_map/source/pallas_call | solution.py:403
  18.9 5.2 %all-to-all-start = ((f32[8,2,296,256]{3,2,1,0:T(8,128)}), f32[8,2,296,256]{3,2,1,0:T(8,128)}, u32[]{:S(2)}, u32[]{:S(2)}) async-start(f32[8,2,296,256]{3,2,1,0:T(8,128)} %source.1), calls=%async_computation | async-start | bytes 9699328 | tf_op jit(solution)/shard_map/all_to_all | solution.py:418
  24.2 0.2 fusion.21.step
  24.4 0.2 fusion.29
  24.6 0.2 fusion.27
  24.8 0.3 fusion.6
  25.1 0.3 fusion.7
  25.4 0.3 fusion.13.coef
  25.7 0.0 copy-start.4
  25.7 53.7 %all-to-all-done.x = f32[8,2,296,256]{3,2,1,0:T(8,128)} async-done(((f32[8,2,296,256]{3,2,1,0:T(8,128)}), f32[8,2,296,256]{3,2,1,0:T(8,128)}, u32[]{:S(2)}, u32[]{:S(2)}) %all-to-all-start) | async-done | bytes 4849696 | tf_op jit(solution)/shard_map/all_to_all | solution.py:418
  79.4 0.0 copy-done.4
  79.4 12.8 %forward.1 = (f32[2,9,256,256]{3,2,1,0:T(8,128)}, f32[2,256,256]{2,1,0:T(8,128)}, f32[2,256,256]{2,1,0:T(8,128)}) custom-call(f32[8,2,296,256]{3,2,1,0:T(8,128)} %all-to-all-done.x, f32[256,256]{1,0:T(8,128)} %add_multiply_fusion.4.table, f32[5,256,256]{2,1,0:T(8,128)} %copy-done.4), custom_call_target="tpu_custom_call" | custom-call | tf_op jit(solution)/shard_map/forward/pallas_call | solution.py:424
  92.2 0.0 copy-start.2
  92.2 1.0 copy-done.2
  93.3 0.0 copy-start.3
  93.3 1.0 copy-done.3
  94.3 22.8 %carry.1 = (f32[2,256,256]{2,1,0:T(8,128)S(1)}, f32[2,256,256]{2,1,0:T(8,128)S(1)}) custom-call(f32[2,256,256]{2,1,0:T(8,128)S(1)} %copy-done.2, f32[2,256,256]{2,1,0:T(8,128)S(1)} %copy-done.3, f32[256,256]{1,0:T(8,128)S(1)} %fusion.21.step), custom_call_target="tpu_custom_call" | custom-call | tf_op jit(solution)/shard_map/carry/pallas_call | solution.py:442
  117.1 0.0 copy-start
  117.2 0.8 copy-done
  118.0 0.0 copy-start.1
  118.0 0.8 copy-done.1
  118.8 13.3 %backward.1 = f32[8,2,296,256]{3,2,1,0:T(8,128)} custom-call(f32[2,9,256,256]{3,2,1,0:T(8,128)} %get-tuple-element.7.modes, f32[2,256,256]{2,1,0:T(8,128)} %copy-done, f32[2,256,256]{2,1,0:T(8,128)} %copy-done.1, f32[256,256]{1,0:T(8,128)} %add_multiply_fusion.4.table, f32[5,256,256]{2,1,0:T(8,128)} %copy-done.4), custom_call_target="tpu_custom_call" | custom-call | tf_op jit(solution)/shard_map/backward/pallas_call | solution.py:455
  132.1 61.0 %all_to_all.10.x = f32[8,2,296,256]{3,2,1,0:T(8,128)} all-to-all(f32[8,2,296,256]{3,2,1,0:T(8,128)} %backward.1), channel_id=1, replica_groups=mesh['grp'=2,'px'=4,'py'=4] {'grp','px'}, dimensions={0} | all-to-all | bytes 9699328 | tf_op jit(solution)/shard_map/all_to_all | solution.py:472
  193.1 28.4 %project.1 = (f32[3,8,16,32,256]{4,3,2,1,0:T(8,128)}, f32[3,8,16,32,256]{4,3,2,1,0:T(8,128)}) custom-call(f32[8,2,296,256]{3,2,1,0:T(8,128)} %all_to_all.10.x, f32[3,8,16,32,256]{4,3,2,1,0:T(8,128)} %mult.3, f32[256,256]{1,0:T(8,128)} %add_multiply_fusion.4.table), custom_call_target="tpu_custom_call" | custom-call | tf_op jit(solution)/shard_map/project/pallas_call | solution.py:475
  (1 shorter events, 0.0 us)
Async XLA Ops:
  18.9 60.5 %all-to-all-start = ((f32[8,2,296,256]{3,2,1,0:T(8,128)}), f32[8,2,296,256]{3,2,1,0:T(8,128)}, u32[]{:S(2)}, u32[]{:S(2)}) async-start(f32[8,2,296,256]{3,2,1,0:T(8,128)} %source.1), calls=%async_computation | async-start | bytes 9699328 | tf_op jit(solution)/shard_map/all_to_all | solution.py:418
  25.7 53.7 %copy-start.4 = (f32[5,256,256]{2,1,0:T(8,128)}, f32[5,256,256]{2,1,0:T(8,128)S(1)}, u32[]{:S(2)}) copy-start(f32[5,256,256]{2,1,0:T(8,128)S(1)} %fusion.13.coef) | copy-start | bytes 3932164
  92.2 1.0 copy-start.2
  93.3 1.0 copy-start.3
  117.1 0.8 copy-start
  118.0 0.8 copy-start.1
where the time goes:
time: 222 us; the launch traced here: 221 us
  Pallas kernels  93.9 us (42%)
  blocking collectives  61 us (27%)
  waiting for transfers between devices  53.7 us (24%)
  starting transfers between devices  5.18 us (2%)
  local copies, waits for them, and re-layouts  3.68 us (2%)
  other arithmetic  3.3 us (1%)
    all_to_all x1, blocking collectives, local(): lax.all_to_all(returned, SPACE, split_axis=0, concat_axis=0, tiled=True)  61 us
    all_to_all x1, waiting for transfers between devices, local(): lax.all_to_all(payload, SPACE, split_axis=0, concat_axis=0, tiled=True)  53.7 us
    pallas_call x1, Pallas kernels, local(): pl.pallas_call(functools.partial(project_kernel, levels=levels), out_shap...  28.4 us
    pallas_call x1, Pallas kernels, local(): pl.pallas_call(functools.partial(carry_kernel, blocks=blocks, pieces=piec...  22.8 us
    pallas_call x1, Pallas kernels, local(): pl.pallas_call(functools.partial(source_kernel, levels=levels), out_shape...  16.6 us
    pallas_call x1, Pallas kernels, local(): pl.pallas_call(functools.partial(backward_kernel, here=here, rows=rows, l...  13.3 us
    pallas_call x1, Pallas kernels, local(): pl.pallas_call(functools.partial(forward_kernel, here=here, rows=rows), o...  12.8 us
    all_to_all x1, starting transfers between devices, local(): lax.all_to_all(payload, SPACE, split_axis=0, concat_axis=0, tiled=True)  5.18 us
  transfers between devices with their start and end apart: 1, of which 1 were waited for; matrix products, arithmetic and copies ran while one was open for 1% of the time, Pallas kernels for 0%

commit v1 on v0

v1 whole, which is shorter than its diff:
```python
import functools
import math

import jax
import jax.numpy as jnp
import ml_dtypes
import numpy as np
from jax import lax
from jax.experimental import pallas as pl
from jax.experimental.pallas import tpu as pltpu
from jax.sharding import PartitionSpec as P

NEWTON = 4
PENALTY = 1.0
VMEM_LIMIT = 60 * 1024 * 1024
SPACE = ("grp", "px")
EVERY = ("grp", "px", "py")
MESH = pl.DeviceIdType.MESH
bf16 = jnp.bfloat16
f32 = jnp.float32


def halves(table):
    high = table.astype(ml_dtypes.bfloat16)
    low = (table - high.astype(np.float64)).astype(ml_dtypes.bfloat16)
    return np.stack([high, low])


def hartley(length):
    angles = 2.0 * np.pi / length * (np.outer(np.arange(length), np.arange(length)) % length)
    return (np.cos(angles) + np.sin(angles)) / np.sqrt(length)


def cosines(length):
    k = np.arange(length)[:, None]
    x = np.arange(length)[None, :]
    weights = np.where(k == 0, np.sqrt(1.0 / length), np.sqrt(2.0 / length))
    return weights * np.cos(np.pi * k * (2 * x + 1) / (2 * length))


def slab_tables(rows, cols, here, blocks):
    j = np.arange(rows)[:, None]
    n = np.arange(cols)[None, :]
    lam = 4.0 * np.sin(np.pi * j / (2 * rows)) ** 2 + 4.0 * np.sin(np.pi * n / cols) ** 2
    sinh = np.sqrt(lam * (1.0 + 0.25 * lam))
    ratio = 1.0 / (1.0 + 0.5 * lam + sinh)
    positive = lam > 0.0
    full = ratio ** (2 * here * blocks)
    scale = np.where(positive, 0.5 / np.where(positive, sinh * (1.0 - full), 1.0), 0.0)
    edge = cosines(rows)[:, :1]
    low, high, down, low_q, high_q = [], [], [], [], []
    for block in range(blocks):
        first = block * here
        lows = [1.0 + ratio ** (2 * (first + v) + 1) for v in range(here + 1)]
        highs = [1.0 + ratio ** (2.0 * (blocks * here - 1 - first - v) + 1.0) for v in range(here + 1)]
        low.append(lows)
        high.append(highs)
        down.append([ratio**v * highs[v] for v in range(here + 1)])
        low_q.append([edge * ratio ** (here - v) * lows[v] for v in range(here)])
        high_q.append([edge * ratio**v * highs[v] for v in range(here)])
    single = np.stack([ratio, ratio**here, scale, edge * scale, np.broadcast_to(edge, lam.shape)])
    pack = lambda parts: np.asarray(parts, np.float32)
    per_block = np.concatenate(
        [pack(low), pack(high), pack(down), pack(low_q), pack(high_q)], axis=1
    )
    return single.astype(np.float32), per_block


def ring_tables(rows, cols, group, levels):
    r = np.arange(group)[:, None, None]
    k = np.arange(levels)[None, :, None]
    n = np.arange(cols)[None, None, :]
    tau = 4.0 * np.sin(np.pi * k / (2 * levels)) ** 2
    kappa = tau + 4.0 * np.sin(np.pi * n / cols) ** 2
    turn = 2.0 * np.sin(np.pi * r / group) ** 2
    positive = kappa > 0.0
    safe = np.where(positive, kappa, 1.0)
    shrink = 1.0 / (1.0 + 0.5 * safe + np.sqrt(safe * (1.0 + 0.25 * safe)))
    far = shrink**rows
    inverse = (1.0 - shrink) * (1.0 - far * far) / (
        (1.0 + shrink) * ((1.0 - far) ** 2 + 2.0 * far * turn)
    )
    inverse = np.where(positive, inverse, np.where(r == 0, 1.0 / rows, 0.0))
    edge = math.sqrt(1.0 / rows)
    flat = inverse[:, :, :1]
    moving = edge * flat / np.where(tau > 0.0, tau, 1.0)
    still = rows * edge / np.where(r > 0, 2.0 * turn, 1.0) * (r > 0)
    extra = np.where(tau > 0.0, moving, still)
    mix = np.kron(hartley(group), cosines(levels))
    flat_rows = group * levels
    return (
        mix.astype(np.float32),
        inverse.reshape(flat_rows, cols).astype(np.float32),
        extra.reshape(flat_rows, 1).astype(np.float32),
    )


def split(x):
    high = x.astype(bf16)
    return high, (x - high.astype(f32)).astype(bf16)


def mm(a, b):
    return jnp.dot(a, b, preferred_element_type=f32)


def times_table(x, table):
    high, low = split(x)
    return mm(high, table[0]) + (mm(low, table[0]) + mm(high, table[1]))


def table_times(table, x):
    high, low = split(x)
    return mm(table[0], high) + (mm(table[0], low) + mm(table[1], high))


def precise(a, b):
    return jnp.dot(a, b, precision=lax.Precision.HIGHEST, preferred_element_type=f32)


def over_rows(table, x, out):
    problems, rows, cols = x.shape
    size = table.shape[1]
    bunch = size // rows
    for g in range(problems // bunch):
        part = x[g * bunch : (g + 1) * bunch].reshape(size, cols)
        out[g * bunch : (g + 1) * bunch] = table_times(table, part).reshape(bunch, rows, cols)


def source_kernel(
    mult, aux, start, end, col_table, row_table, single, per_block,
    modes, up, down, rims, prev, body, tail, *, levels, here
):
    t = pl.program_id(0)
    problems, rows, cols = body.shape
    level = lax.axis_index("py") * here + t
    row = lax.broadcasted_iota(jnp.int32, (rows, cols), 0)

    @pl.when(t == 0)
    def _():
        prev[...] = jnp.zeros_like(prev)
        tail[...] = jnp.zeros_like(tail)
        up[...] = jnp.zeros_like(up)
        down[...] = jnp.zeros_like(down)

    @pl.when(t < here)
    def _():
        keep = jnp.where(level == levels - 1, 0.0, 1.0)
        begin = jnp.where(level == 0, -1.0 / PENALTY, 0.0)
        finish = jnp.where(level == levels - 1, 1.0 / PENALTY, 0.0)

        def one(b, carry):
            along = aux[1, 0, b] - mult[1, 0, b] / PENALTY
            tail[b, pl.ds(t, 1), :] = along[rows - 1 :, :]
            beside = jnp.where(row == 0, 0.0, pltpu.roll(along, 1, 0))
            along = jnp.where(row == rows - 1, 0.0, along)
            second = aux[2, 0, b] - mult[2, 0, b] / PENALTY
            across = pltpu.roll(second, 1, 1) - second
            now = (aux[0, 0, b] - mult[0, 0, b] / PENALTY) * keep
            boundary = begin * start[b] + finish * end[b]
            body[b] = prev[b] - now + beside - along + across + boundary
            prev[b] = now
            return carry

        lax.fori_loop(0, problems, one, 0, unroll=4)

    @pl.when(t == here)
    def _():
        body[...] = prev[...]
        held = tail.shape[1]
        flat = tail[...].reshape(problems * held, cols)
        rims[...] = times_table(flat, col_table).reshape(problems, held, cols)

    spread = times_table(body[...].reshape(problems * rows, cols), col_table)
    over_rows(row_table, spread.reshape(problems, rows, cols), modes.at[0])
    ratio = single[0]
    low = per_block[t]
    falling = per_block[2 * (here + 1) + t]

    def add(b, carry):
        value = modes[0, b]
        up[b] = ratio * up[b] + low * value
        down[b] = down[b] + falling * value
        return carry

    lax.fori_loop(0, problems, add, 0, unroll=4)


def carry_kernel(up_own, down_own, step, up_in, down_in, up_got, down_got, up_out, down_out,
                 up_sent, up_came, down_sent, down_came, *, blocks, pieces, lag):
    me = lax.axis_index("py")
    size = up_own.shape[0] // pieces
    has_lower = me > 0
    has_upper = me < blocks - 1

    def copy(source, target, sent, came, k, other):
        cut = pl.ds(k * size, size)
        return pltpu.make_async_remote_copy(
            src_ref=source.at[cut],
            dst_ref=target.at[cut],
            send_sem=sent.at[k],
            recv_sem=came.at[k],
            device_id={"py": other},
            device_id_type=MESH,
        )

    barrier = pltpu.get_barrier_semaphore()

    @pl.when(has_lower)
    def _():
        pl.semaphore_signal(barrier, inc=1, device_id={"py": me - 1}, device_id_type=MESH)

    @pl.when(has_upper)
    def _():
        pl.semaphore_signal(barrier, inc=1, device_id={"py": me + 1}, device_id_type=MESH)

    @pl.when(has_lower & has_upper)
    def _():
        pl.semaphore_wait(barrier, 2)

    @pl.when(jnp.logical_not(has_lower & has_upper))
    def _():
        pl.semaphore_wait(barrier, 1)

    def relay(k, own, got, out, sent, came, first, last, ahead):
        cut = pl.ds(k * size, size)

        @pl.when(jnp.logical_not(first))
        def _():
            copy(out, got, sent, came, k, ahead).wait_recv()

            @pl.when(jnp.logical_not(last))
            def _():
                out[cut] = own[cut] + step[...] * got[cut]
                copy(out, got, sent, came, k, ahead).start()

    up = (up_own, up_got, up_out, up_sent, up_came, me == 0, me == blocks - 1,
          (me + 1) % blocks)
    down = (down_own, down_got, down_out, down_sent, down_came, me == blocks - 1, me == 0,
            (me + blocks - 1) % blocks)

    @pl.when(me == 0)
    def _():
        for k in range(pieces):
            copy(up_own, up_got, up_sent, up_came, k, me + 1).start()

    @pl.when(me == blocks - 1)
    def _():
        for k in range(pieces):
            copy(down_own, down_got, down_sent, down_came, k, me - 1).start()

    def weave(early, late):
        for k in range(pieces + lag):
            if k < pieces:
                relay(k, *early)
            if k >= lag:
                relay(k - lag, *late)

    lower_half = me < blocks // 2

    @pl.when(lower_half)
    def _():
        weave(up, down)

    @pl.when(jnp.logical_not(lower_half))
    def _():
        weave(down, up)

    @pl.when(has_lower)
    def _():
        up_in[...] = up_got[...]
        for k in range(pieces):
            copy(down_out, down_got, down_sent, down_came, k, me - 1).wait_send()

    @pl.when(me == 0)
    def _():
        up_in[...] = jnp.zeros_like(up_in)

    @pl.when(has_upper)
    def _():
        down_in[...] = down_got[...]
        for k in range(pieces):
            copy(up_out, up_got, up_sent, up_came, k, me + 1).wait_send()

    @pl.when(me == blocks - 1)
    def _():
        down_in[...] = jnp.zeros_like(down_in)


def trace_kernel(modes, up, down, rims, single, per_block, pay, *, here):
    _, problems, rows, cols = modes.shape
    lane = lax.broadcasted_iota(jnp.int32, (1, cols), 1)
    parity = lax.broadcasted_iota(jnp.int32, (8, cols), 0) % 2 == 0

    def one(b, carry):
        total = [jnp.zeros((8, cols), f32) for _ in range(here)]
        for c in range(rows // 8):
            cut = slice(c * 8, c * 8 + 8)
            ratio, weight = single[0, cut, :], single[3, cut, :]
            lows = [per_block[v, cut, :] for v in range(here + 1)]
            highs = [per_block[here + 1 + v, cut, :] for v in range(here + 1)]
            value = up[b, cut, :]
            sums = []
            for v in range(here):
                if v:
                    value = ratio * value
                value = value + lows[v] * modes[v, b, cut, :]
                sums.append(highs[v] * value)
            behind = down[b, cut, :]
            for v in range(here, -1, -1):
                if v < here:
                    total[v] = total[v] + weight * (sums[v] + lows[v] * behind)
                behind = ratio * (behind + highs[v] * modes[v, b, cut, :])
        for v in range(here):
            even = jnp.sum(jnp.where(parity, total[v], 0.0), axis=0, keepdims=True)
            odd = jnp.sum(jnp.where(parity, 0.0, total[v]), axis=0, keepdims=True)
            pay[b, v : v + 1, :] = even + odd
            pay[b, here + v : here + v + 1, :] = even - odd + rims[b, v : v + 1, :]
            flat = jnp.where(lane == 0, modes[v, b, 0:1, :], 0.0)
            if v == 0:
                beyond = pltpu.roll(modes[here, b, 0:8, :], 1, 1)[0:1]
                flat = flat + jnp.where(lane == 1, beyond, 0.0)
            pay[b, 2 * here + v : 2 * here + v + 1, :] = flat
        return carry

    lax.fori_loop(0, problems, one, 0)


def ring_kernel(left, right, flat, mix, mix_back, inverse, extra, out, *, here, levels):
    total, width = left.shape
    lane = lax.broadcasted_iota(jnp.int32, (total, width), 1)
    ahead = total - levels
    jump = pltpu.roll(left[...], ahead, 0) - right[...]
    beyond = pltpu.roll(pltpu.roll(flat[...], here, 0), width - 1, 1)
    whole = jnp.where(lane == 0, flat[...] + beyond, 0.0)
    jump_flat = pltpu.roll(whole, ahead, 0) - whole
    solved = precise(mix[...], jump) * inverse[...] + precise(mix[...], jump_flat) * extra[...]
    out[...] = precise(mix_back[...], solved)


def flux_kernel(flux, per_block, up, down, *, here):
    problems, rows, cols = up.shape
    sign = jnp.where(lax.broadcasted_iota(jnp.int32, (rows, cols), 0) % 2 == 0, 1.0, -1.0)
    base = 3 * (here + 1)

    def one(b, carry):
        rise = jnp.zeros((rows, cols), f32)
        fall = jnp.zeros((rows, cols), f32)
        for v in range(here):
            mine = jnp.broadcast_to(flux[b, v : v + 1, :], (rows, cols))
            other = jnp.broadcast_to(flux[b, here + v : here + v + 1, :], (rows, cols))
            both = sign * mine - other
            rise = rise + per_block[base + v] * both
            fall = fall + per_block[base + here + v] * both
        up[b] = rise
        down[b] = fall
        return carry

    lax.fori_loop(0, problems, one, 0)


def project_kernel(
    modes, flux, rims, up1, down1, up2, down2, col_table, row_back, single, per_block, mult,
    next_mult, next_aux, wave, phi, following, edges, *, levels, here
):
    t = pl.program_id(0)
    problems, rows, cols = phi.shape
    first = lax.axis_index("py") * here
    moving = jnp.where(first + t == levels - 1, 0.0, 1.0)

    def field(at, to):
        over_rows(row_back, wave[at], to)
        flat = to[...].reshape(problems * rows, cols)
        to[...] = times_table(flat, col_table).reshape(problems, rows, cols)

    def sweep(b, carry):
        for c in range(rows // 8):
            cut = slice(c * 8, c * 8 + 8)
            ratio, scale, edge = single[0, cut, :], single[2, cut, :], single[4, cut, :]
            sign = jnp.where(
                lax.broadcasted_iota(jnp.int32, (8, cols), 0) % 2 == 0, edge, -edge
            )
            lows = [per_block[v, cut, :] for v in range(here + 1)]
            highs = [per_block[here + 1 + v, cut, :] for v in range(here + 1)]
            value = up1[b, cut, :] + up2[b, cut, :]
            source, sums = [], []
            for v in range(here + 1):
                now = modes[v, b, cut, :]
                if v < here:
                    mine = jnp.broadcast_to(flux[b, v : v + 1, :], (8, cols))
                    other = jnp.broadcast_to(flux[b, here + v : here + v + 1, :], (8, cols))
                    now = now + (sign * mine - edge * other)
                source.append(now)
                if v:
                    value = ratio * value
                value = value + lows[v] * now
                sums.append(highs[v] * value)
            behind = down1[b, cut, :] + down2[b, cut, :]
            for v in range(here, -1, -1):
                wave[v, b, cut, :] = scale * (sums[v] + lows[v] * behind)
                behind = ratio * (behind + highs[v] * source[v])
            if c == 0:
                spot = (lax.broadcasted_iota(jnp.int32, (8, 128), 0) == 0) & (
                    lax.broadcasted_iota(jnp.int32, (8, 128), 1) == 0
                )
                below = 0.5 * (up1[b, 0:8, 0:128] + up2[b, 0:8, 0:128])
                whole = below + 0.5 * (down1[b, 0:8, 0:128] + down2[b, 0:8, 0:128])
                for v in range(here + 1):
                    whole = whole + source[v][:, 0:128]
                mean = whole * (1.0 / levels)
                level_value = jnp.zeros((8, 128), f32)
                for v in range(here + 1):
                    wave[v, b, 0:8, 0:128] = jnp.where(spot, level_value, wave[v, b, 0:8, 0:128])
                    if v < here:
                        below = below + source[v][:, 0:128]
                        count = (first + (v + 1)).astype(f32)
                        level_value = level_value - (below - count * mean)
        return carry

    @pl.when(t == 0)
    def _():
        lax.fori_loop(0, problems, sweep, 0)
        field(0, following)
        held = edges.shape[1]
        flat = (flux[:, 0:here, :] + rims[:, 0:here, :]).reshape(problems * here, cols)
        edges[:, 0:here, :] = times_table(flat, col_table).reshape(problems, here, cols)

    phi[...] = following[...]
    field(t + 1, following)
    row = lax.broadcasted_iota(jnp.int32, (rows, cols), 0)

    def one(b, carry):
        here_phi = phi[b]
        rim = jnp.broadcast_to(edges[b, pl.ds(t, 1), :], (rows, cols))
        grad_time = (following[b] - here_phi) * moving
        grad_first = jnp.where(
            row == rows - 1, rim, pltpu.roll(here_phi, rows - 1, 0) - here_phi
        )
        grad_second = pltpu.roll(here_phi, cols - 1, 1) - here_phi
        mult_time, mult_first, mult_second = (mult[k, 0, b] for k in range(3))
        time_part = grad_time + mult_time / PENALTY
        along = grad_first + mult_first / PENALTY
        beside = grad_second + mult_second / PENALTY
        kinetic = 0.5 * (along * along + beside * beside)
        offset_one = 1.0 + time_part
        solid = kinetic > 1e-37
        root = jnp.exp(jnp.log(jnp.where(solid, kinetic, 1.0)) * (1.0 / 3.0))
        scaling = jnp.maximum(offset_one, 1.0) + jnp.where(solid, root, 0.0)
        twice = 2.0 * offset_one
        for newton_step in range(NEWTON):
            above = scaling * scaling * (2.0 * scaling - offset_one) + kinetic
            derivative = scaling * (3.0 * scaling - twice)
            scaling = jnp.maximum(above / derivative, 1.0)
        feasible = time_part + kinetic <= 0.0
        shrink = jnp.where(feasible, 1.0, 1.0 / scaling)
        out_time = jnp.where(feasible, time_part, time_part - (scaling - 1.0))
        out_along = along * shrink
        out_beside = beside * shrink
        next_aux[0, 0, b] = out_time
        next_aux[1, 0, b] = out_along
        next_aux[2, 0, b] = out_beside
        next_mult[0, 0, b] = mult_time + PENALTY * (grad_time - out_time)
        next_mult[1, 0, b] = mult_first + PENALTY * (grad_first - out_along)
        next_mult[2, 0, b] = mult_second + PENALTY * (grad_second - out_beside)
        return carry

    lax.fori_loop(0, problems, one, 0, unroll=2)


def params():
    return pltpu.CompilerParams(vmem_limit_bytes=VMEM_LIMIT)


def whole_block(shape):
    return pl.BlockSpec(shape, lambda *_: (0,) * len(shape))


def local(multiplier, auxiliary, density_start, density_end):
    _, here, problems, rows, cols = multiplier.shape
    blocks = lax.axis_size("py")
    group = lax.axis_size("grp") * lax.axis_size("px")
    devices = group * blocks
    levels = here * blocks
    held = -(-here // 8) * 8
    bunch = min(problems, max(1, 256 // rows))
    shape = lambda *s: jax.ShapeDtypeStruct(s, f32)

    col_table = jnp.asarray(halves(hartley(cols)))
    cosine = np.kron(np.eye(bunch), cosines(rows))
    row_table = jnp.asarray(halves(cosine))
    row_back = jnp.asarray(halves(cosine.T))
    single, per_block = slab_tables(rows, cols, here, blocks)
    single = jnp.asarray(single)
    me = lax.axis_index("py")
    per_block = lax.dynamic_index_in_dim(jnp.asarray(per_block), me, 0, keepdims=False)
    mix, inverse, extra = ring_tables(rows, cols, group, levels)
    width = problems * cols // devices
    parts = cols // width
    flat_id = lax.axis_index(SPACE) * blocks + me
    slot = flat_id % parts
    inverse = lax.dynamic_slice_in_dim(jnp.asarray(inverse), slot * width, width, 1)
    extra = jnp.where(slot == 0, jnp.asarray(extra), 0.0)

    plane = (problems, rows, cols)
    level_block = pl.BlockSpec(
        (3, 1, problems, rows, cols), lambda t: (0, jnp.minimum(t, here - 1), 0, 0, 0)
    )
    modes, up_own, down_own, rims = pl.pallas_call(
        functools.partial(source_kernel, levels=levels, here=here),
        out_shape=(shape(here + 1, *plane), shape(*plane), shape(*plane),
                   shape(problems, held, cols)),
        grid=(here + 1,),
        in_specs=[level_block, level_block, whole_block(plane), whole_block(plane),
                  whole_block(col_table.shape), whole_block(row_table.shape),
                  whole_block(single.shape), whole_block(per_block.shape)],
        out_specs=(pl.BlockSpec((1, *plane), lambda t: (t, 0, 0, 0)), whole_block(plane),
                   whole_block(plane), whole_block((problems, held, cols))),
        scratch_shapes=[pltpu.VMEM(plane, f32), pltpu.VMEM(plane, f32),
                        pltpu.VMEM((problems, held, cols), f32)],
        compiler_params=params(),
        name="source",
    )(multiplier, auxiliary, density_start, density_end, col_table, row_table, single, per_block)

    vmem = pl.BlockSpec(memory_space=pltpu.VMEM)

    def carry(up, down, which):
        pieces = math.gcd(problems, 8)
        return pl.pallas_call(
            functools.partial(carry_kernel, blocks=blocks, pieces=pieces, lag=min(3, pieces)),
            out_shape=(shape(*plane), shape(*plane)),
            in_specs=[vmem, vmem, vmem],
            out_specs=(vmem, vmem),
            scratch_shapes=[pltpu.VMEM(plane, f32)] * 4 + [pltpu.SemaphoreType.DMA((pieces,))] * 4,
            compiler_params=pltpu.CompilerParams(
                collective_id=which, has_side_effects=True, vmem_limit_bytes=24 * 1024 * 1024
            ),
            name="carry%d" % which,
        )(up, down, single[1])

    up1, down1 = carry(up_own, down_own, 0)

    half = problems // 2
    pay = pl.pallas_call(
        functools.partial(trace_kernel, here=here),
        out_shape=shape(problems, 3 * here, cols),
        grid=(2,),
        in_specs=[pl.BlockSpec((here + 1, half, rows, cols), lambda i: (0, i, 0, 0)),
                  pl.BlockSpec((half, rows, cols), lambda i: (i, 0, 0)),
                  pl.BlockSpec((half, rows, cols), lambda i: (i, 0, 0)),
                  pl.BlockSpec((half, held, cols), lambda i: (i, 0, 0)),
                  whole_block(single.shape), whole_block(per_block.shape)],
        out_specs=pl.BlockSpec((half, 3 * here, cols), lambda i: (i, 0, 0)),
        compiler_params=params(),
        name="trace",
    )(modes, up1, down1, rims, single, per_block)

    pay = pay.reshape(problems, 3 * here, parts, width).transpose(0, 2, 1, 3)
    pay = pay.reshape(devices, 3 * here, width)
    pay = lax.all_to_all(pay, EVERY, split_axis=0, concat_axis=0, tiled=True)
    pay = pay.reshape(devices, 3, here, width).transpose(1, 0, 2, 3).reshape(3, devices * here, width)
    total = devices * here

    flux = pl.pallas_call(
        functools.partial(ring_kernel, here=here, levels=levels),
        out_shape=shape(total, width),
        compiler_params=params(),
        name="ring",
    )(pay[0], pay[1], pay[2], jnp.asarray(mix), jnp.asarray(mix.T.copy()), inverse, extra)

    flux = jnp.stack([flux, jnp.roll(flux, levels, axis=0)])
    flux = flux.reshape(2, devices, here, width).transpose(1, 0, 2, 3).reshape(devices, 2 * here, width)
    flux = lax.all_to_all(flux, EVERY, split_axis=0, concat_axis=0, tiled=True)
    flux = flux.reshape(problems, parts, 2 * here, width).transpose(0, 2, 1, 3)
    flux = flux.reshape(problems, 2 * here, cols)

    up2, down2 = pl.pallas_call(
        functools.partial(flux_kernel, here=here),
        out_shape=(shape(*plane), shape(*plane)),
        compiler_params=params(),
        name="flux",
    )(flux, per_block)
    up2, down2 = carry(up2, down2, 1)

    once = lambda s: pl.BlockSpec(s, lambda t: (0,) * len(s), pipeline_mode=pl.Buffered(1))
    out_shape = shape(*multiplier.shape)
    level_block = pl.BlockSpec((3, 1, problems, rows, cols), lambda t: (0, t, 0, 0, 0))
    return pl.pallas_call(
        functools.partial(project_kernel, levels=levels, here=here),
        out_shape=(out_shape, out_shape),
        grid=(here,),
        in_specs=[once((here + 1, *plane)), once(flux.shape), once(rims.shape), once(plane),
                  once(plane), once(plane), once(plane), once(col_table.shape),
                  once(row_back.shape), once(single.shape), once(per_block.shape), level_block],
        out_specs=(level_block, level_block),
        scratch_shapes=[pltpu.VMEM((here + 1, *plane), f32), pltpu.VMEM(plane, f32),
                        pltpu.VMEM(plane, f32), pltpu.VMEM((problems, held, cols), f32)],
        compiler_params=params(),
        name="project",
    )(modes, flux, rims, up1, down1, up2, down2, col_table, row_back, single, per_block, multiplier)


def solution(mesh):
    placed = (
        P(None, "py", None, ("grp", "px"), None),
        P(None, "py", None, ("grp", "px"), None),
        P(None, ("grp", "px"), None),
        P(None, ("grp", "px"), None),
    )
    return jax.shard_map(
        local,
        mesh=mesh,
        in_specs=placed,
        out_specs=(
            P(None, "py", None, ("grp", "px"), None),
            P(None, "py", None, ("grp", "px"), None),
        ),
        check_vma=False,
    )
```

time: 222 us -> 159 us (0.72)
  blocking collectives: 61 us -> 13.8 us
  waiting for transfers between devices: 53.7 us -> 10.5 us
  Pallas kernels: 93.9 us -> 111 us
  local copies, waits for them, and re-layouts: 3.68 us -> 14.9 us
    all_to_all x1, blocking collectives: 61 us -> 13.8 us  [local(): flux = lax.all_to_all(flux, EVERY, split_axis=0, concat_axis=0, tiled=True)]
    all_to_all x1, waiting for transfers between devices: 53.7 us -> 10.5 us  [local(): pay = lax.all_to_all(pay, EVERY, split_axis=0, concat_axis=0, tiled=True)]
    pallas_call x5 -> x7, Pallas kernels: 93.9 us -> 111 us  [the longest x2 45.5 us: carry(): pl.pallas_call(functools.partial(carry_kernel, blocks=blocks, pieces=piec...]
    unnamed x10 -> x22, local copies, waits for them, and re-layouts: 3.68 us -> 7.4 us
    squeeze x0 -> x2, local copies, waits for them, and re-layouts: none -> 3.38 us  [the longest x1 2.63 us: local(): lax.dynamic_index_in_dim(jnp.asarray(per_block), me, 0, keepdims=False)]
where the time goes in v1:
time: 159 us; the launch traced here: 158 us
  Pallas kernels  111 us (70%)
  local copies, waits for them, and re-layouts  14.9 us (9%)
  blocking collectives  13.8 us (9%)
  waiting for transfers between devices  10.5 us (7%)
  starting transfers between devices  4.73 us (3%)
  other arithmetic  2.37 us (1%)
    pallas_call x2, Pallas kernels, carry(): pl.pallas_call(functools.partial(carry_kernel, blocks=blocks, pieces=piec...  45.5 us
    pallas_call x1, Pallas kernels, local(): pl.pallas_call(functools.partial(project_kernel, levels=levels, here=here...  33.4 us
    pallas_call x1, Pallas kernels, local(): pl.pallas_call(functools.partial(source_kernel, levels=levels, here=here)...  20 us
    all_to_all x1, blocking collectives, local(): flux = lax.all_to_all(flux, EVERY, split_axis=0, concat_axis=0, tiled=True)  13.8 us
    all_to_all x1, waiting for transfers between devices, local(): pay = lax.all_to_all(pay, EVERY, split_axis=0, concat_axis=0, tiled=True)  10.5 us
    unnamed x22, local copies, waits for them, and re-layouts  7.4 us
    pallas_call x1, Pallas kernels, local(): pl.pallas_call(functools.partial(trace_kernel, here=here), out_shape=shap...  5.51 us
    all_to_all x1, starting transfers between devices, local(): pay = lax.all_to_all(pay, EVERY, split_axis=0, concat_axis=0, tiled=True)  4.73 us
  transfers between devices with their start and end apart: 1, of which 1 were waited for; matrix products, arithmetic and copies ran while one was open for 1% of the time, Pallas kernels for 0%

profile of v1, /device:TPU:0, one launch (start us, length us, event | category | flops | bytes accessed | tf_op | source)
XLA Modules:
  0.0 158.0 jit_solution(9049317892637970339)
XLA Ops:
  0.6 2.6 %dynamic-slice_bitcast_fusion.per_block = f32[43,32,256]{2,1,0:T(8,128)} fusion(f32[4,43,32,256]{3,2,1,0:T(8,128)} %constant.61.clone, s32[]{:T(128)S(6)} %select_n.22), kind=kLoop, calls=%fused_computation | loop fusion | bytes 2818052 | tf_op jit(solution)/shard_map/jit(dynamic_index_in_dim)/squeeze | solution.py:495
  3.3 20.0 %source.1 = (f32[9,16,32,256]{3,2,1,0:T(8,128)}, f32[16,32,256]{2,1,0:T(8,128)}, f32[16,32,256]{2,1,0:T(8,128)}, f32[16,8,256]{2,1,0:T(8,128)}) custom-call(f32[3,8,16,32,256]{4,3,2,1,0:T(8,128)} %mult.3, f32[3,8,16,32,256]{4,3,2,1,0:T(8,128)} %aux.1, f32[16,32,256]{2,1,0:T(8,128)} %start.1, f32[16,32,256]{2,1,0:T(8,128)} %end.1, ...), custom_call_target="tpu_custom_call" | custom-call | tf_op jit(solution)/shard_map/source/pallas_call | solution.py:508
  23.3 0.0 copy-done.8
  23.3 0.0 copy-start.4
  23.3 1.0 copy-done.4
  24.3 1.0 copy-done.5
  25.4 23.9 %carry0.1 = (f32[16,32,256]{2,1,0:T(8,128)S(1)}, f32[16,32,256]{2,1,0:T(8,128)S(1)}) custom-call(f32[16,32,256]{2,1,0:T(8,128)S(1)} %copy-done.4, f32[16,32,256]{2,1,0:T(8,128)S(1)} %copy-done.5, f32[32,256]{1,0:T(8,128)S(1)} %copy-done.8), custom_call_target="tpu_custom_call" | custom-call | tf_op jit(solution)/shard_map/carry0/pallas_call | solution.py:528
  49.3 0.0 copy-start
  49.3 0.8 copy-done
  50.1 0.8 copy-done.1
  50.9 5.5 %trace.1 = f32[16,24,256]{2,1,0:T(8,128)} custom-call(f32[9,16,32,256]{3,2,1,0:T(8,128)} %get-tuple-element.12.modes, f32[16,32,256]{2,1,0:T(8,128)} %copy-done, f32[16,32,256]{2,1,0:T(8,128)} %copy-done.1, f32[16,8,256]{2,1,0:T(8,128)} %get-tuple-element.17.rims, f32[5,32,256]{2,1,0:T(8,128)} %constant.60.clone.single, ...), custom_call_target="tpu_custom_call" | custom-call | tf_op jit(solution)/shard_map/trace/pallas_call | solution.py:543
  56.4 1.0 fusion
  57.5 0.8 pad_maximum_fusion
  58.2 4.7 %all-to-all-start = ((f32[32,24,128]{2,1,0:T(8,128)}), f32[32,24,128]{2,1,0:T(8,128)S(1)}, u32[]{:S(2)}, u32[]{:S(2)}) async-start(f32[32,24,128]{2,1,0:T(8,128)} %bitcast.1), calls=%async_computation | async-start | bytes 786432 | tf_op jit(solution)/shard_map/all_to_all | solution.py:559
  63.0 0.7 constant_dynamic-slice_fusion.inverse
  63.7 0.0 copy-done.9
  63.7 0.7 broadcast_select_fusion.extra
  64.3 10.5 %all-to-all-done = f32[32,24,128]{2,1,0:T(8,128)S(1)} async-done(((f32[32,24,128]{2,1,0:T(8,128)}), f32[32,24,128]{2,1,0:T(8,128)S(1)}, u32[]{:S(2)}, u32[]{:S(2)}) %all-to-all-start) | async-done | bytes 393248 | tf_op jit(solution)/shard_map/all_to_all | solution.py:559
  74.8 0.7 slice_bitcast_fusion
  75.6 3.2 %ring.1 = f32[256,128]{1,0:T(8,128)} custom-call(f32[256,128]{1,0:T(8,128)} %get-tuple-element.24.left, f32[256,128]{1,0:T(8,128)} %get-tuple-element.23.right, f32[256,128]{1,0:T(8,128)} %get-tuple-element.22.flat, f32[256,256]{1,0:T(8,128)} %constant.64.clone.mix, f32[256,256]{1,0:T(8,128)} %constant.65.clone.mix_back, ...), custom_call_target="tpu_custom_call" | custom-call | tf_op jit(solution)/shard_map/ring/pallas_call | solution.py:563
  78.8 0.7 slice.43
  79.5 0.9 slice.44
  80.5 0.9 maximum_bitcast_fusion
  81.4 13.8 %all_to_all.10 = f32[32,16,128]{2,1,0:T(8,128)S(1)} all-to-all(f32[32,16,128]{2,1,0:T(8,128)S(1)} %maximum_bitcast_fusion), channel_id=1, replica_groups=mesh['grp'=2,'px'=4,'py'=4] {'grp','px','py'}, dimensions={0} | all-to-all | bytes 524288 | tf_op jit(solution)/shard_map/all_to_all | solution.py:572
  95.2 0.7 copy.20
  96.0 3.3 %flux.1 = (f32[16,32,256]{2,1,0:T(8,128)}, f32[16,32,256]{2,1,0:T(8,128)}) custom-call(f32[16,16,256]{2,1,0:T(8,128)} %bitcast.30, f32[43,32,256]{2,1,0:T(8,128)} %dynamic-slice_bitcast_fusion.per_block), custom_call_target="tpu_custom_call" | custom-call | tf_op jit(solution)/shard_map/flux/pallas_call | solution.py:576
  99.3 1.0 copy-done.6
  100.3 1.0 copy-done.7
  101.4 21.6 %carry1.1 = (f32[16,32,256]{2,1,0:T(8,128)S(1)}, f32[16,32,256]{2,1,0:T(8,128)S(1)}) custom-call(f32[16,32,256]{2,1,0:T(8,128)S(1)} %copy-done.6, f32[16,32,256]{2,1,0:T(8,128)S(1)} %copy-done.7, f32[32,256]{1,0:T(8,128)S(1)} %copy-done.8), custom_call_target="tpu_custom_call" | custom-call | tf_op jit(solution)/shard_map/carry1/pallas_call | solution.py:528
  123.0 0.8 copy-done.2
  123.8 0.8 copy-done.3
  124.6 33.4 %project.1 = (f32[3,8,16,32,256]{4,3,2,1,0:T(8,128)}, f32[3,8,16,32,256]{4,3,2,1,0:T(8,128)}) custom-call(f32[9,16,32,256]{3,2,1,0:T(8,128)} %get-tuple-element.12.modes, f32[16,16,256]{2,1,0:T(8,128)} %bitcast.31, f32[16,8,256]{2,1,0:T(8,128)} %get-tuple-element.17.rims, f32[16,32,256]{2,1,0:T(8,128)} %copy-done, f32[16,32,256]{2,1,0:T(8,128)} %copy-done.1, ...), custom_call_target="tpu_custom_call" | custom-call | tf_op jit(solution)/shard_map/project/pallas_call | solution.py:587
  (11 shorter events, 0.0 us)
Async XLA Ops:
  3.3 20.0 %copy-start.8 = (f32[32,256]{1,0:T(8,128)S(1)}, f32[32,256]{1,0:T(8,128)}, u32[]{:S(2)}) copy-start(f32[32,256]{1,0:T(8,128)} %constant.67.step) | copy-start | bytes 98308
  23.3 1.0 copy-start.4
  24.3 1.0 copy-start.5
  25.4 37.6 %copy-start.10 = (f32[256,256]{1,0:T(8,128)S(1)}, f32[256,256]{1,0:T(8,128)}, u32[]{:S(2)}) copy-start(f32[256,256]{1,0:T(8,128)} %constant.62.clone) | copy-start | bytes 786436
  25.4 38.3 %copy-start.9 = (f32[256,1]{1,0:T(8,128)S(1)}, f32[256,1]{1,0:T(8,128)}, u32[]{:S(2)}) copy-start(f32[256,1]{1,0:T(8,128)} %constant.63.clone) | copy-start | bytes 3076
  49.3 0.8 copy-start
  50.1 0.8 copy-start.1
  58.2 16.6 %all-to-all-start = ((f32[32,24,128]{2,1,0:T(8,128)}), f32[32,24,128]{2,1,0:T(8,128)S(1)}, u32[]{:S(2)}, u32[]{:S(2)}) async-start(f32[32,24,128]{2,1,0:T(8,128)} %bitcast.1), calls=%async_computation | async-start | bytes 786432 | tf_op jit(solution)/shard_map/all_to_all | solution.py:559
  99.3 1.0 copy-start.6
  100.3 1.0 copy-start.7
  123.0 0.8 copy-start.2
  123.8 0.9 copy-start.3

commit v2 on v1

v2 whole, which is shorter than its diff:
```python
import functools
import math

import jax
import jax.numpy as jnp
import ml_dtypes
import numpy as np
from jax import lax
from jax.experimental import pallas as pl
from jax.experimental.pallas import tpu as pltpu
from jax.sharding import PartitionSpec as P

NEWTON = 4
PENALTY = 1.0
VMEM_LIMIT = 60 * 1024 * 1024
SPACE = ("grp", "px")
EVERY = ("grp", "px", "py")
MESH = pl.DeviceIdType.MESH
bf16 = jnp.bfloat16
f32 = jnp.float32


def halves(table):
    high = table.astype(ml_dtypes.bfloat16)
    low = (table - high.astype(np.float64)).astype(ml_dtypes.bfloat16)
    return np.stack([high, low])


def hartley(length):
    angles = 2.0 * np.pi / length * (np.outer(np.arange(length), np.arange(length)) % length)
    return (np.cos(angles) + np.sin(angles)) / np.sqrt(length)


def cosines(length):
    k = np.arange(length)[:, None]
    x = np.arange(length)[None, :]
    weights = np.where(k == 0, np.sqrt(1.0 / length), np.sqrt(2.0 / length))
    return weights * np.cos(np.pi * k * (2 * x + 1) / (2 * length))


def slab_tables(rows, cols, here, blocks):
    j = np.arange(rows)[:, None]
    n = np.arange(cols)[None, :]
    lam = 4.0 * np.sin(np.pi * j / (2 * rows)) ** 2 + 4.0 * np.sin(np.pi * n / cols) ** 2
    sinh = np.sqrt(lam * (1.0 + 0.25 * lam))
    ratio = 1.0 / (1.0 + 0.5 * lam + sinh)
    positive = lam > 0.0
    full = ratio ** (2 * here * blocks)
    scale = np.where(positive, 0.5 / np.where(positive, sinh * (1.0 - full), 1.0), 0.0)
    edge = cosines(rows)[:, :1]
    low, high, down, low_q, high_q = [], [], [], [], []
    for block in range(blocks):
        first = block * here
        lows = [1.0 + ratio ** (2 * (first + v) + 1) for v in range(here + 1)]
        highs = [1.0 + ratio ** (2.0 * (blocks * here - 1 - first - v) + 1.0) for v in range(here + 1)]
        low.append(lows)
        high.append(highs)
        down.append([ratio**v * highs[v] for v in range(here + 1)])
        low_q.append([edge * ratio ** (here - v) * lows[v] for v in range(here)])
        high_q.append([edge * ratio**v * highs[v] for v in range(here)])
    single = np.stack([ratio, ratio**here, scale, edge * scale, np.broadcast_to(edge, lam.shape)])
    pack = lambda parts: np.asarray(parts, np.float32)
    ahead = np.concatenate([pack(low), pack(high), pack(down)], axis=1)
    after = np.concatenate([pack(low), pack(high), pack(low_q), pack(high_q)], axis=1)
    return single.astype(np.float32), ahead, after


def ring_tables(rows, cols, group, levels):
    r = np.arange(group)[:, None, None]
    k = np.arange(levels)[None, :, None]
    n = np.arange(cols)[None, None, :]
    tau = 4.0 * np.sin(np.pi * k / (2 * levels)) ** 2
    kappa = tau + 4.0 * np.sin(np.pi * n / cols) ** 2
    turn = 2.0 * np.sin(np.pi * r / group) ** 2
    positive = kappa > 0.0
    safe = np.where(positive, kappa, 1.0)
    shrink = 1.0 / (1.0 + 0.5 * safe + np.sqrt(safe * (1.0 + 0.25 * safe)))
    far = shrink**rows
    inverse = (1.0 - shrink) * (1.0 - far * far) / (
        (1.0 + shrink) * ((1.0 - far) ** 2 + 2.0 * far * turn)
    )
    inverse = np.where(positive, inverse, np.where(r == 0, 1.0 / rows, 0.0))
    edge = math.sqrt(1.0 / rows)
    flat = inverse[:, :, :1]
    moving = edge * flat / np.where(tau > 0.0, tau, 1.0)
    still = rows * edge / np.where(r > 0, 2.0 * turn, 1.0) * (r > 0)
    extra = np.where(tau > 0.0, moving, still)
    mix = np.kron(hartley(group), cosines(levels))
    flat_rows = group * levels
    return (
        mix.astype(np.float32),
        inverse.reshape(flat_rows, cols).astype(np.float32),
        extra.reshape(flat_rows, 1).astype(np.float32),
    )


def split(x):
    high = x.astype(bf16)
    return high, (x - high.astype(f32)).astype(bf16)


def mm(a, b):
    return jnp.dot(a, b, preferred_element_type=f32)


def times_table(x, table):
    high, low = split(x)
    return mm(high, table[0]) + (mm(low, table[0]) + mm(high, table[1]))


def table_times(table, x):
    high, low = split(x)
    return mm(table[0], high) + (mm(table[0], low) + mm(table[1], high))


def precise(a, b):
    return jnp.dot(a, b, precision=lax.Precision.HIGHEST, preferred_element_type=f32)


def over_rows(table, x):
    units, rows, cols = x.shape
    size = table.shape[1]
    bunch = size // rows
    parts = []
    for g in range(units // bunch):
        part = x[g * bunch : (g + 1) * bunch].reshape(size, cols)
        parts.append(table_times(table, part).reshape(bunch, rows, cols))
    return parts[0] if len(parts) == 1 else jnp.concatenate(parts, axis=0)


def steps_from(me, blocks):
    return me, blocks - 1 - me


class Chain:
    def __init__(self, up, down, step, size, blocks):
        self.me = lax.axis_index("py")
        self.blocks, self.size, self.step = blocks, size, step
        self.far = steps_from(self.me, blocks)
        self.next = ((self.me + 1) % blocks, (self.me + blocks - 1) % blocks)
        self.refs = (up, down)

    def copy(self, way, source, k):
        _, got, _, sent, came = self.refs[way]
        cut = pl.ds(k * self.size, self.size)
        return pltpu.make_async_remote_copy(
            src_ref=source.at[cut],
            dst_ref=got.at[cut],
            send_sem=sent.at[k],
            recv_sem=came.at[k],
            device_id={"py": self.next[way]},
            device_id_type=MESH,
        )

    def greet(self):
        barrier = pltpu.get_barrier_semaphore()
        lower, upper = self.me > 0, self.me < self.blocks - 1

        @pl.when(lower)
        def _():
            pl.semaphore_signal(barrier, inc=1, device_id={"py": self.me - 1}, device_id_type=MESH)

        @pl.when(upper)
        def _():
            pl.semaphore_signal(barrier, inc=1, device_id={"py": self.me + 1}, device_id_type=MESH)

        @pl.when(lower & upper)
        def _():
            pl.semaphore_wait(barrier, 2)

        @pl.when(jnp.logical_not(lower & upper))
        def _():
            pl.semaphore_wait(barrier, 1)

    def clear(self):
        for way in range(2):
            got = self.refs[way][1]

            @pl.when(self.far[way] == 0)
            def _():
                got[...] = jnp.zeros_like(got)

    def begin(self, k):
        for way in range(2):

            @pl.when(self.far[way] == 0)
            def _():
                self.copy(way, self.refs[way][0], k).start()

    def relay(self, way, k, low, high):
        own, got, out, _, _ = self.refs[way]

        @pl.when((self.far[way] > 0) & (k >= low) & (k < high))
        def _():
            self.copy(way, out, k).wait_recv()

            @pl.when(self.far[way] < self.blocks - 1)
            def _():
                for q in range(self.size):
                    at = k * self.size + q
                    out[at] = own[at] + self.step[...] * got[at]
                self.copy(way, out, k).start()

    def finish(self, pieces):
        for way in range(2):

            @pl.when(self.far[way] < self.blocks - 1)
            def _():
                def one(k, carry):
                    self.copy(way, self.refs[way][2], k).wait_send()
                    return carry

                lax.fori_loop(0, pieces, one, 0)


def trace_problem(b, modes, up, down, rims, single, tables, pay, *, here):
    rows, cols = up.shape[1], up.shape[2]
    width = pay.shape[3]
    parts = cols // width
    lane = lax.broadcasted_iota(jnp.int32, (1, cols), 1)
    parity = lax.broadcasted_iota(jnp.int32, (8, cols), 0) % 2 == 0
    total = [jnp.zeros((8, cols), f32) for _ in range(here)]
    for c in range(rows // 8):
        cut = slice(c * 8, c * 8 + 8)
        ratio, weight = single[0, cut, :], single[3, cut, :]
        value = up[b, cut, :]
        sums = []
        for v in range(here):
            if v:
                value = ratio * value
            value = value + tables[v, cut, :] * modes[v, b, cut, :]
            sums.append(tables[here + 1 + v, cut, :] * value)
        behind = down[b, cut, :]
        for v in range(here, -1, -1):
            if v < here:
                total[v] = total[v] + weight * (sums[v] + tables[v, cut, :] * behind)
            behind = ratio * (behind + tables[here + 1 + v, cut, :] * modes[v, b, cut, :])

    def put(kind, v, row):
        for n in range(parts):
            pay[b * parts + n, kind, v : v + 1, :] = row[:, n * width : (n + 1) * width]

    for v in range(here):
        even = jnp.sum(jnp.where(parity, total[v], 0.0), axis=0, keepdims=True)
        odd = jnp.sum(jnp.where(parity, 0.0, total[v]), axis=0, keepdims=True)
        put(0, v, even + odd)
        put(1, v, even - odd + rims[b, v : v + 1, :])
        flat = jnp.where(lane == 0, modes[v, b, 0:1, :], 0.0)
        if v == 0:
            beyond = pltpu.roll(modes[here, b, 0:8, :], 1, 1)[0:1]
            flat = flat + jnp.where(lane == 1, beyond, 0.0)
        put(2, v, flat)


def source_kernel(
    mult, aux, start, end, col_table, row_table, single, tables_all,
    modes_out, up_all, down_all, rims, pay,
    modes, prev, body, tail, tables, up_own, down_own, up_got, down_got, up_out, down_out,
    up_sent, up_came, down_sent, down_came, moved, table_sem,
    *, levels, here, blocks, chunks, pieces, delay
):
    chunk_index, t = pl.program_id(0), pl.program_id(1)
    chunk, rows, cols = body.shape
    steps = here + 1
    g = chunk_index * steps + t
    me = lax.axis_index("py")
    level = me * here + t
    base = chunk_index * chunk
    size = chunk // pieces
    row = lax.broadcasted_iota(jnp.int32, (rows, cols), 0)
    chain = Chain(
        (up_own, up_got, up_out, up_sent, up_came),
        (down_own, down_got, down_out, down_sent, down_came),
        single.at[1], size, blocks,
    )
    fetch = pltpu.make_async_copy(tables_all.at[me], tables, table_sem)

    @pl.when(g == 0)
    def _():
        fetch.start()
        chain.clear()
        chain.greet()

    @pl.when(t == 0)
    def _():
        prev[...] = jnp.zeros_like(prev)
        tail[...] = jnp.zeros_like(tail)
        up_own[pl.ds(base, chunk)] = jnp.zeros((chunk, rows, cols), f32)
        down_own[pl.ds(base, chunk)] = jnp.zeros((chunk, rows, cols), f32)

    @pl.when(t < here)
    def _():
        keep = jnp.where(level == levels - 1, 0.0, 1.0)
        begin = jnp.where(level == 0, -1.0 / PENALTY, 0.0)
        finish = jnp.where(level == levels - 1, 1.0 / PENALTY, 0.0)

        def one(b, carry):
            along = aux[1, 0, b] - mult[1, 0, b] / PENALTY
            tail[b, pl.ds(t, 1), :] = along[rows - 1 :, :]
            beside = jnp.where(row == 0, 0.0, pltpu.roll(along, 1, 0))
            along = jnp.where(row == rows - 1, 0.0, along)
            second = aux[2, 0, b] - mult[2, 0, b] / PENALTY
            across = pltpu.roll(second, 1, 1) - second
            now = (aux[0, 0, b] - mult[0, 0, b] / PENALTY) * keep
            boundary = begin * start[b] + finish * end[b]
            body[b] = prev[b] - now + beside - along + across + boundary
            prev[b] = now
            return carry

        lax.fori_loop(0, chunk, one, 0, unroll=4)

    @pl.when(t == here)
    def _():
        body[...] = prev[...]
        held = tail.shape[1]
        flat = tail[...].reshape(chunk * held, cols)
        rims[pl.ds(base, chunk)] = times_table(flat, col_table).reshape(chunk, held, cols)

    spread = times_table(body[...].reshape(chunk * rows, cols), col_table)
    modes[t, pl.ds(base, chunk)] = over_rows(row_table, spread.reshape(chunk, rows, cols))

    @pl.when(g == 0)
    def _():
        fetch.wait()

    ratio = single[0]
    low = tables[t]
    falling = tables[2 * steps + t]

    def add(b, carry):
        value = modes[t, b]
        up_own[b] = ratio * up_own[b] + low * value
        down_own[b] = down_own[b] + falling * value
        return carry

    lax.fori_loop(base, base + chunk, add, 0)

    def relays(at, owner):
        for way in range(2):
            k = at - ((owner + 1) * steps - 1) - delay * chain.far[way]
            chain.relay(way, k + owner * pieces, owner * pieces, (owner + 1) * pieces)

    for owner in range(chunks - 1):
        relays(g, owner)

    def move(c):
        cut = pl.ds(c * chunk, chunk)
        return pltpu.make_async_copy(modes.at[:, cut], modes_out.at[:, cut], moved.at[c])

    @pl.when(t == here)
    def _():
        move(chunk_index).start()

        def one(k, carry):
            chain.begin(chunk_index * pieces + k)
            return carry

        lax.fori_loop(0, pieces, one, 0)

    @pl.when(g == chunks * steps - 1)
    def _():
        final = chunks * steps - 1
        reach = delay * (blocks - 1)
        open_at = [max(1, (owner + 1) * steps - 1 + reach - final) for owner in range(chunks)]

        def slot(i, carry):
            for owner in range(chunks):
                if (owner + 1) * steps - 1 + reach + pieces - 1 > final:
                    relays(final + i, owner)
            for owner in range(chunks):
                k = i - open_at[owner]

                @pl.when((k >= 0) & (k < pieces))
                def _():
                    def one(q, carry):
                        trace_problem(
                            (owner * pieces + k) * size + q, modes, up_got, down_got, rims,
                            single, tables, pay, here=here,
                        )
                        return carry

                    lax.fori_loop(0, size, one, 0)

            return carry

        lax.fori_loop(1, max(open_at) + pieces, slot, 0)
        ups = pltpu.make_async_copy(up_got, up_all, moved.at[chunks])
        downs = pltpu.make_async_copy(down_got, down_all, moved.at[chunks + 1])
        ups.start()
        downs.start()
        chain.finish(chunks * pieces)
        ups.wait()
        downs.wait()
        for c in range(chunks):
            move(c).wait()


def sweep_problem(b, modes, flux, up1, up2, down1, down2, single, tables, wave, *, here, levels):
    rows, cols = up1.shape[1], up1.shape[2]
    first = lax.axis_index("py") * here
    for c in range(rows // 8):
        cut = slice(c * 8, c * 8 + 8)
        ratio, scale, edge = single[0, cut, :], single[2, cut, :], single[4, cut, :]
        sign = jnp.where(
            lax.broadcasted_iota(jnp.int32, (8, cols), 0) % 2 == 0, edge, -edge
        )
        value = up1[b, cut, :] + up2[b, cut, :]
        source, sums = [], []
        for v in range(here + 1):
            now = modes[v, b, cut, :]
            if v < here:
                mine = jnp.broadcast_to(flux[b, v : v + 1, :], (8, cols))
                other = jnp.broadcast_to(flux[b, here + v : here + v + 1, :], (8, cols))
                now = now + (sign * mine - edge * other)
            source.append(now)
            if v:
                value = ratio * value
            value = value + tables[v, cut, :] * now
            sums.append(tables[here + 1 + v, cut, :] * value)
        behind = down1[b, cut, :] + down2[b, cut, :]
        for v in range(here, -1, -1):
            wave[v, b, cut, :] = scale * (sums[v] + tables[v, cut, :] * behind)
            behind = ratio * (behind + tables[here + 1 + v, cut, :] * source[v])
        if c == 0:
            spot = (lax.broadcasted_iota(jnp.int32, (8, 128), 0) == 0) & (
                lax.broadcasted_iota(jnp.int32, (8, 128), 1) == 0
            )
            below = 0.5 * (up1[b, 0:8, 0:128] + up2[b, 0:8, 0:128])
            whole = below + 0.5 * (down1[b, 0:8, 0:128] + down2[b, 0:8, 0:128])
            for v in range(here + 1):
                whole = whole + source[v][:, 0:128]
            mean = whole * (1.0 / levels)
            level_value = jnp.zeros((8, 128), f32)
            for v in range(here + 1):
                wave[v, b, 0:8, 0:128] = jnp.where(spot, level_value, wave[v, b, 0:8, 0:128])
                if v < here:
                    below = below + source[v][:, 0:128]
                    count = (first + (v + 1)).astype(f32)
                    level_value = level_value - (below - count * mean)


def flux_problem(b, flux, tables, up, down, *, here):
    rows, cols = up.shape[1], up.shape[2]
    sign = jnp.where(lax.broadcasted_iota(jnp.int32, (rows, cols), 0) % 2 == 0, 1.0, -1.0)
    base = 2 * (here + 1)
    rise = jnp.zeros((rows, cols), f32)
    fall = jnp.zeros((rows, cols), f32)
    for v in range(here):
        mine = jnp.broadcast_to(flux[b, v : v + 1, :], (rows, cols))
        other = jnp.broadcast_to(flux[b, here + v : here + v + 1, :], (rows, cols))
        both = sign * mine - other
        rise = rise + tables[base + v] * both
        fall = fall + tables[base + here + v] * both
    up[b] = rise
    down[b] = fall


def flat_rows(ref, kind, here):
    devices, width = ref.shape[0], ref.shape[3]
    if here % 8 == 0:
        return ref[:, kind].reshape(devices * here, width)
    return jnp.concatenate([ref[i, kind] for i in range(devices)], axis=0)


def solve_kernel(
    pay, modes_all, up_all, down_all, rims, single, tables_all, mix, mix_back, ring,
    col_table, row_back,
    phi_all, edges,
    recv, back, came, flux, modes, wave, tables, up1, down1,
    up_own, down_own, up_got, down_got, up_out, down_out,
    up_sent, up_came, down_sent, down_came, sent1, came1, sent2, came2, loaded, moved,
    *, levels, here, blocks, group, inner, pieces, delay
):
    problems, rows, cols = up1.shape
    devices, width = pay.shape[0], pay.shape[3]
    parts = cols // width
    size = problems // pieces
    me_py = lax.axis_index("py")
    me = (lax.axis_index("grp") * inner + lax.axis_index("px")) * blocks + me_py
    chain = Chain(
        (up_own, up_got, up_out, up_sent, up_came),
        (down_own, down_got, down_out, down_sent, down_came),
        single.at[1], size, blocks,
    )

    def place(i):
        other = (me + i) % devices
        where = {
            "grp": other // (inner * blocks),
            "px": other // blocks % inner,
            "py": other % blocks,
        }
        return other, where

    loads = [
        pltpu.make_async_copy(modes_all, modes, loaded.at[0]),
        pltpu.make_async_copy(up_all, up1, loaded.at[1]),
        pltpu.make_async_copy(down_all, down1, loaded.at[2]),
        pltpu.make_async_copy(tables_all.at[me_py], tables, loaded.at[3]),
    ]

    barrier = pltpu.get_barrier_semaphore()

    def hail(i, carry):
        _, where = place(i)
        pl.semaphore_signal(barrier, inc=1, device_id=where, device_id_type=MESH)
        return carry

    lax.fori_loop(1, devices, hail, 0)
    for load in loads:
        load.start()
    chain.clear()
    pl.semaphore_wait(barrier, devices - 1)

    def exchange(source, target, sent, arrived, i):
        other, where = place(i)
        return pltpu.make_async_remote_copy(
            src_ref=source.at[other],
            dst_ref=target.at[me],
            send_sem=sent.at[i],
            recv_sem=arrived.at[i],
            device_id=where,
            device_id_type=MESH,
        )

    def every(action):
        def one(i, carry):
            action(i)
            return carry

        lax.fori_loop(1, devices, one, 0)

    first = lambda i: exchange(pay, recv, sent1, came1, i)
    second = lambda i: exchange(back, came, sent2, came2, i)
    every(lambda i: first(i).start())
    recv[me] = pay[me]
    every(lambda i: first(i).wait_recv())

    total = devices * here
    lane = lax.broadcasted_iota(jnp.int32, (total, width), 1)
    slot_id = me % parts
    jump = pltpu.roll(flat_rows(recv, 0, here), total - levels, 0) - flat_rows(recv, 1, here)
    flat = flat_rows(recv, 2, here)
    beyond = pltpu.roll(pltpu.roll(flat, here, 0), width - 1, 1)
    whole = jnp.where(lane == 0, flat + beyond, 0.0)
    jump_flat = pltpu.roll(whole, total - levels, 0) - whole
    solved = precise(mix[...], jump) * ring[0, slot_id]
    solved = solved + precise(mix[...], jump_flat) * ring[1, slot_id]
    mine = precise(mix_back[...], solved)
    other = pltpu.roll(mine, levels, 0)
    if here % 8 == 0:
        back[:, 0] = mine.reshape(devices, here, width)
        back[:, 1] = other.reshape(devices, here, width)
    else:
        for i in range(devices):
            back[i, 0] = mine[i * here : (i + 1) * here]
            back[i, 1] = other[i * here : (i + 1) * here]
    every(lambda i: second(i).start())
    came[me] = back[me]
    every(lambda i: second(i).wait_recv())
    for i in range(devices):
        b, n = i // parts, i % parts
        for kind in range(2):
            flux[b, kind * here : (kind + 1) * here, n * width : (n + 1) * width] = came[i, kind]
    for load in loads:
        load.wait()

    reach = delay * (blocks - 1)

    def send_out(k):
        cut = pl.ds(k * size, size)
        return pltpu.make_async_copy(
            wave.at[pl.ds(0, here), cut], phi_all.at[pl.ds(0, here), cut], moved.at[k]
        )

    def slot(i, carry):
        @pl.when(i < pieces)
        def _():
            def one(q, carry):
                flux_problem(i * size + q, flux, tables, up_own, down_own, here=here)
                return carry

            lax.fori_loop(0, size, one, 0)
            chain.begin(i)

        for way in range(2):
            chain.relay(way, i - delay * chain.far[way], 0, pieces)

        k = i - reach

        @pl.when(k >= 0)
        def _():
            def one(q, carry):
                sweep_problem(
                    k * size + q, modes, flux, up1, up_got, down1, down_got, single, tables,
                    wave, here=here, levels=levels,
                )
                return carry

            lax.fori_loop(0, size, one, 0)
            cut = pl.ds(k * size, size)
            part = over_rows(row_back, wave[0:here, cut].reshape(here * size, rows, cols))
            part = times_table(part.reshape(here * size * rows, cols), col_table)
            wave[0:here, cut] = part.reshape(here, size, rows, cols)
            send_out(k).start()

        return carry

    lax.fori_loop(0, pieces + reach, slot, 0)
    last = over_rows(row_back, wave[here])
    last = times_table(last.reshape(problems * rows, cols), col_table)
    wave[here] = last.reshape(problems, rows, cols)
    tip = pltpu.make_async_copy(wave.at[here], phi_all.at[here], moved.at[pieces])
    tip.start()
    if here % 8 == 0:
        rim = (flux[:, 0:here, :] + rims[:, 0:here, :]).reshape(problems * here, cols)
        edges[...] = times_table(rim, col_table).reshape(problems, here, cols)
    else:
        for b in range(problems):
            edges[b] = times_table(flux[b, 0:here, :] + rims[b, 0:here, :], col_table)
    chain.finish(pieces)
    every(lambda i: first(i).wait_send())
    every(lambda i: second(i).wait_send())
    for k in range(pieces):
        send_out(k).wait()
    tip.wait()


def project_kernel(phi, following, edges, mult, next_mult, next_aux, *, levels):
    t = pl.program_id(0)
    here = pl.num_programs(0)
    _, problems, rows, cols = phi.shape
    moving = jnp.where(lax.axis_index("py") * here + t == levels - 1, 0.0, 1.0)
    row = lax.broadcasted_iota(jnp.int32, (rows, cols), 0)

    def one(b, carry):
        here_phi = phi[0, b]
        rim = jnp.broadcast_to(edges[b, pl.ds(t, 1), :], (rows, cols))
        grad_time = (following[0, b] - here_phi) * moving
        grad_first = jnp.where(
            row == rows - 1, rim, pltpu.roll(here_phi, rows - 1, 0) - here_phi
        )
        grad_second = pltpu.roll(here_phi, cols - 1, 1) - here_phi
        mult_time, mult_first, mult_second = (mult[k, 0, b] for k in range(3))
        time_part = grad_time + mult_time / PENALTY
        along = grad_first + mult_first / PENALTY
        beside = grad_second + mult_second / PENALTY
        kinetic = 0.5 * (along * along + beside * beside)
        offset_one = 1.0 + time_part
        solid = kinetic > 1e-37
        root = jnp.exp(jnp.log(jnp.where(solid, kinetic, 1.0)) * (1.0 / 3.0))
        scaling = jnp.maximum(offset_one, 1.0) + jnp.where(solid, root, 0.0)
        twice = 2.0 * offset_one
        for newton_step in range(NEWTON):
            above = scaling * scaling * (2.0 * scaling - offset_one) + kinetic
            derivative = scaling * (3.0 * scaling - twice)
            scaling = jnp.maximum(above / derivative, 1.0)
        feasible = time_part + kinetic <= 0.0
        shrink = jnp.where(feasible, 1.0, 1.0 / scaling)
        out_time = jnp.where(feasible, time_part, time_part - (scaling - 1.0))
        out_along = along * shrink
        out_beside = beside * shrink
        next_aux[0, 0, b] = out_time
        next_aux[1, 0, b] = out_along
        next_aux[2, 0, b] = out_beside
        next_mult[0, 0, b] = mult_time + PENALTY * (grad_time - out_time)
        next_mult[1, 0, b] = mult_first + PENALTY * (grad_first - out_along)
        next_mult[2, 0, b] = mult_second + PENALTY * (grad_second - out_beside)
        return carry

    lax.fori_loop(0, problems, one, 0, unroll=2)


def params(which=None):
    if which is None:
        return pltpu.CompilerParams(vmem_limit_bytes=VMEM_LIMIT)
    return pltpu.CompilerParams(
        collective_id=which, has_side_effects=True, vmem_limit_bytes=VMEM_LIMIT
    )


def whole_block(shape):
    return pl.BlockSpec(shape, lambda *_: (0,) * len(shape))


def local(multiplier, auxiliary, density_start, density_end):
    _, here, problems, rows, cols = multiplier.shape
    blocks = lax.axis_size("py")
    inner = lax.axis_size("px")
    group = lax.axis_size("grp") * inner
    devices = group * blocks
    levels = here * blocks
    held = -(-here // 8) * 8
    width = problems * cols // devices
    parts = cols // width
    shape = lambda *s: jax.ShapeDtypeStruct(s, f32)
    vector = lambda *s: pltpu.VMEM(s, f32)
    anywhere = pl.BlockSpec(memory_space=pl.ANY)
    vmem = pl.BlockSpec(memory_space=pltpu.VMEM)
    dma = lambda n: pltpu.SemaphoreType.DMA((n,))
    delay = 2

    chunks = 2
    chunk = problems // chunks
    pieces = math.gcd(chunk, 4)
    bunch = math.gcd(chunk, max(1, 256 // rows))
    col_table = jnp.asarray(halves(hartley(cols)))
    row_table = jnp.asarray(halves(np.kron(np.eye(bunch), cosines(rows))))
    single, ahead, after = slab_tables(rows, cols, here, blocks)
    single, ahead, after = jnp.asarray(single), jnp.asarray(ahead), jnp.asarray(after)

    plane = (problems, rows, cols)
    level_block = pl.BlockSpec(
        (3, 1, chunk, rows, cols), lambda c, t: (0, jnp.minimum(t, here - 1), c, 0, 0)
    )
    density_block = pl.BlockSpec((chunk, rows, cols), lambda c, t: (c, 0, 0))
    modes, up1, down1, rims, pay = pl.pallas_call(
        functools.partial(source_kernel, levels=levels, here=here, blocks=blocks, chunks=chunks,
                          pieces=pieces, delay=delay),
        out_shape=(shape(here + 1, *plane), shape(*plane), shape(*plane),
                   shape(problems, held, cols), shape(devices, 3, here, width)),
        grid=(chunks, here + 1),
        in_specs=[level_block, level_block, density_block, density_block,
                  whole_block(col_table.shape), whole_block(row_table.shape),
                  whole_block(single.shape), anywhere],
        out_specs=(anywhere, anywhere, anywhere, whole_block((problems, held, cols)),
                   whole_block((devices, 3, here, width))),
        scratch_shapes=[vector(here + 1, *plane), vector(chunk, rows, cols),
                        vector(chunk, rows, cols), vector(chunk, held, cols),
                        vector(*ahead.shape[1:])] + [vector(*plane)] * 6
        + [dma(chunks * pieces)] * 4 + [dma(chunks + 2), pltpu.SemaphoreType.DMA],
        compiler_params=params(0),
        name="source",
    )(multiplier, auxiliary, density_start, density_end, col_table, row_table, single, ahead)

    mix, inverse, extra = ring_tables(rows, cols, group, levels)
    total = devices * here
    wide = np.zeros((total, cols), np.float32)
    wide[:, :1] = extra
    ring = np.stack([inverse, wide]).reshape(2, total, parts, width).transpose(0, 2, 1, 3).copy()
    pieces = math.gcd(problems, 8)
    size = problems // pieces
    bunch = math.gcd(math.gcd(size * here, problems), max(1, 256 // rows))
    row_back = jnp.asarray(halves(np.kron(np.eye(bunch), cosines(rows).T)))
    phi, edges = pl.pallas_call(
        functools.partial(solve_kernel, levels=levels, here=here, blocks=blocks, group=group,
                          inner=inner, pieces=pieces, delay=delay),
        out_shape=(shape(here + 1, *plane), shape(problems, here, cols)),
        in_specs=[vmem, anywhere, anywhere, anywhere, vmem, vmem, anywhere, vmem, vmem, vmem,
                  vmem, vmem],
        out_specs=(anywhere, vmem),
        scratch_shapes=[vector(devices, 3, here, width), vector(devices, 2, here, width),
                        vector(devices, 2, here, width), vector(problems, 2 * here, cols),
                        vector(here + 1, *plane), vector(here + 1, *plane),
                        vector(*after.shape[1:])] + [vector(*plane)] * 8
        + [dma(pieces)] * 4 + [dma(devices)] * 4 + [dma(4), dma(pieces + 1)],
        compiler_params=params(1),
        name="solve",
    )(pay, modes, up1, down1, rims, single, after, jnp.asarray(mix), jnp.asarray(mix.T.copy()),
      jnp.asarray(ring), col_table, row_back)

    out_shape = shape(*multiplier.shape)
    level_block = pl.BlockSpec((3, 1, *plane), lambda t: (0, t, 0, 0, 0))
    phi_block = pl.BlockSpec((1, *plane), lambda t: (t, 0, 0, 0))
    next_block = pl.BlockSpec((1, *plane), lambda t: (t + 1, 0, 0, 0))
    return pl.pallas_call(
        functools.partial(project_kernel, levels=levels),
        out_shape=(out_shape, out_shape),
        grid=(here,),
        in_specs=[phi_block, next_block, whole_block(edges.shape), level_block],
        out_specs=(level_block, level_block),
        compiler_params=params(),
        name="project",
    )(phi, phi, edges, multiplier)


def solution(mesh):
    placed = (
        P(None, "py", None, ("grp", "px"), None),
        P(None, "py", None, ("grp", "px"), None),
        P(None, ("grp", "px"), None),
        P(None, ("grp", "px"), None),
    )
    return jax.shard_map(
        local,
        mesh=mesh,
        in_specs=placed,
        out_specs=(
            P(None, "py", None, ("grp", "px"), None),
            P(None, "py", None, ("grp", "px"), None),
        ),
        check_vma=False,
    )
```

time: 159 us -> 126 us (0.79)
  local copies, waits for them, and re-layouts: 14.9 us -> 0 us
  Pallas kernels: 111 us -> 125 us
  blocking collectives: 13.8 us -> 0 us
  waiting for transfers between devices: 10.5 us -> 0 us
  starting transfers between devices: 4.73 us -> 0 us
  other arithmetic: 2.37 us -> 0 us
    all_to_all x1 -> x0, blocking collectives: 13.8 us -> none  [local(): flux = lax.all_to_all(flux, EVERY, split_axis=0, concat_axis=0, tiled=True)]
    pallas_call x7 -> x3, Pallas kernels: 111 us -> 125 us  [the longest x1 52.7 us: local(): pl.pallas_call(functools.partial(solve_kernel, levels=levels, here=here,...]
    all_to_all x1 -> x0, waiting for transfers between devices: 10.5 us -> none  [local(): pay = lax.all_to_all(pay, EVERY, split_axis=0, concat_axis=0, tiled=True)]
    unnamed x22 -> x0, local copies, waits for them, and re-layouts: 7.4 us -> none
    all_to_all x1 -> x0, starting transfers between devices: 4.73 us -> none  [local(): pay = lax.all_to_all(pay, EVERY, split_axis=0, concat_axis=0, tiled=True)]
    squeeze x2 -> x0, local copies, waits for them, and re-layouts: 3.38 us -> none  [the longest x1 2.63 us: local(): lax.dynamic_index_in_dim(jnp.asarray(per_block), me, 0, keepdims=False)]
    slice x2 -> x0, local copies, waits for them, and re-layouts: 1.62 us -> none  [local(): flux = jnp.stack([flux, jnp.roll(flux, levels, axis=0)])]
  transfers between devices with their start and end apart: 1 -> 0, of which waited for: 1 -> 0; matrix products, arithmetic and copies ran while one was open for 1% -> 0% of each run, Pallas kernels for 0% -> 0%
where the time goes in v2:
time: 126 us; the launch traced here: 125 us
  Pallas kernels  125 us (99%)
    pallas_call x1, Pallas kernels, local(): pl.pallas_call(functools.partial(solve_kernel, levels=levels, here=here,...  52.7 us
    pallas_call x1, Pallas kernels, local(): pl.pallas_call(functools.partial(source_kernel, levels=levels, here=here,...  48 us
    pallas_call x1, Pallas kernels, local(): pl.pallas_call(functools.partial(project_kernel, levels=levels), out_shap...  23.9 us

profile of v2, /device:TPU:0, one launch (start us, length us, event | category | flops | bytes accessed | tf_op | source)
XLA Modules:
  0.0 125.2 jit_solution(16245304941619170245)
XLA Ops:
  0.6 48.0 %source.1 = (f32[9,16,32,256]{3,2,1,0:T(8,128)}, f32[16,32,256]{2,1,0:T(8,128)}, f32[16,32,256]{2,1,0:T(8,128)}, f32[16,8,256]{2,1,0:T(8,128)}, f32[32,3,8,128]{3,2,1,0:T(8,128)}) custom-call(f32[3,8,16,32,256]{4,3,2,1,0:T(8,128)} %mult.3, f32[3,8,16,32,256]{4,3,2,1,0:T(8,128)} %aux.1, f32[16,32,256]{2,1,0:T(8,128)} %start.1, f32[16,32,256]{2,1,0:T(8,128)} %end.1, ...), custom_call_target="tpu_custom_call" | custom-call | tf_op jit(solution)/shard_map/source/pallas_call | solution.py:717
  48.6 52.7 %solve.1 = (f32[9,16,32,256]{3,2,1,0:T(8,128)}, f32[16,8,256]{2,1,0:T(8,128)}) custom-call(f32[32,3,8,128]{3,2,1,0:T(8,128)} %get-tuple-element.9.pay, f32[9,16,32,256]{3,2,1,0:T(8,128)} %get-tuple-element.10.modes_all, f32[16,32,256]{2,1,0:T(8,128)} %get-tuple-element.11.up_all, f32[16,32,256]{2,1,0:T(8,128)} %get-tuple-element.12.down_all, ...), custom_call_target="tpu_custom_call" | custom-call | tf_op jit(solution)/shard_map/solve/pallas_call | solution.py:745
  101.3 23.9 %project.1 = (f32[3,8,16,32,256]{4,3,2,1,0:T(8,128)}, f32[3,8,16,32,256]{4,3,2,1,0:T(8,128)}) custom-call(f32[9,16,32,256]{3,2,1,0:T(8,128)} %get-tuple-element.14.phi.following, f32[9,16,32,256]{3,2,1,0:T(8,128)} %get-tuple-element.14.phi.following, f32[16,8,256]{2,1,0:T(8,128)} %get-tuple-element.15.edges, f32[3,8,16,32,256]{4,3,2,1,0:T(8,128)} %mult.3), custom_call_target="tpu_custom_call" | custom-call | tf_op jit(solution)/shard_map/project/pallas_call | solution.py:766

commit v3 on v2

--- a/solution.py
+++ b/solution.py
@@ -1,5 +1,6 @@
 import functools
 import math
+import types
 
 import jax
 import jax.numpy as jnp
@@ -250,149 +251,6 @@
             beyond = pltpu.roll(modes[here, b, 0:8, :], 1, 1)[0:1]
             flat = flat + jnp.where(lane == 1, beyond, 0.0)
         put(2, v, flat)
-
-
-def source_kernel(
-    mult, aux, start, end, col_table, row_table, single, tables_all,
-    modes_out, up_all, down_all, rims, pay,
-    modes, prev, body, tail, tables, up_own, down_own, up_got, down_got, up_out, down_out,
-    up_sent, up_came, down_sent, down_came, moved, table_sem,
-    *, levels, here, blocks, chunks, pieces, delay
-):
-    chunk_index, t = pl.program_id(0), pl.program_id(1)
-    chunk, rows, cols = body.shape
-    steps = here + 1
-    g = chunk_index * steps + t
-    me = lax.axis_index("py")
-    level = me * here + t
-    base = chunk_index * chunk
-    size = chunk // pieces
-    row = lax.broadcasted_iota(jnp.int32, (rows, cols), 0)
-    chain = Chain(
-        (up_own, up_got, up_out, up_sent, up_came),
-        (down_own, down_got, down_out, down_sent, down_came),
-        single.at[1], size, blocks,
-    )
-    fetch = pltpu.make_async_copy(tables_all.at[me], tables, table_sem)
-
-    @pl.when(g == 0)
-    def _():
-        fetch.start()
-        chain.clear()
-        chain.greet()
-
-    @pl.when(t == 0)
-    def _():
-        prev[...] = jnp.zeros_like(prev)
-        tail[...] = jnp.zeros_like(tail)
-        up_own[pl.ds(base, chunk)] = jnp.zeros((chunk, rows, cols), f32)
-        down_own[pl.ds(base, chunk)] = jnp.zeros((chunk, rows, cols), f32)
-
-    @pl.when(t < here)
-    def _():
-        keep = jnp.where(level == levels - 1, 0.0, 1.0)
-        begin = jnp.where(level == 0, -1.0 / PENALTY, 0.0)
-        finish = jnp.where(level == levels - 1, 1.0 / PENALTY, 0.0)
-
-        def one(b, carry):
-            along = aux[1, 0, b] - mult[1, 0, b] / PENALTY
-            tail[b, pl.ds(t, 1), :] = along[rows - 1 :, :]
-            beside = jnp.where(row == 0, 0.0, pltpu.roll(along, 1, 0))
-            along = jnp.where(row == rows - 1, 0.0, along)
-            second = aux[2, 0, b] - mult[2, 0, b] / PENALTY
-            across = pltpu.roll(second, 1, 1) - second
-            now = (aux[0, 0, b] - mult[0, 0, b] / PENALTY) * keep
-            boundary = begin * start[b] + finish * end[b]
-            body[b] = prev[b] - now + beside - along + across + boundary
-            prev[b] = now
-            return carry
-
-        lax.fori_loop(0, chunk, one, 0, unroll=4)
-
-    @pl.when(t == here)
-    def _():
-        body[...] = prev[...]
-        held = tail.shape[1]
-        flat = tail[...].reshape(chunk * held, cols)
-        rims[pl.ds(base, chunk)] = times_table(flat, col_table).reshape(chunk, held, cols)
-
-    spread = times_table(body[...].reshape(chunk * rows, cols), col_table)
-    modes[t, pl.ds(base, chunk)] = over_rows(row_table, spread.reshape(chunk, rows, cols))
-
-    @pl.when(g == 0)
-    def _():
-        fetch.wait()
-
-    ratio = single[0]
-    low = tables[t]
-    falling = tables[2 * steps + t]
-
-    def add(b, carry):
-        value = modes[t, b]
-        up_own[b] = ratio * up_own[b] + low * value
-        down_own[b] = down_own[b] + falling * value
-        return carry
-
-    lax.fori_loop(base, base + chunk, add, 0)
-
-    def relays(at, owner):
-        for way in range(2):
-            k = at - ((owner + 1) * steps - 1) - delay * chain.far[way]
-            chain.relay(way, k + owner * pieces, owner * pieces, (owner + 1) * pieces)
-
-    for owner in range(chunks - 1):
-        relays(g, owner)
-
-    def move(c):
-        cut = pl.ds(c * chunk, chunk)
-        return pltpu.make_async_copy(modes.at[:, cut], modes_out.at[:, cut], moved.at[c])
-
-    @pl.when(t == here)
-    def _():
-        move(chunk_index).start()
-
-        def one(k, carry):
-            chain.begin(chunk_index * pieces + k)
-            return carry
-
-        lax.fori_loop(0, pieces, one, 0)
-
-    @pl.when(g == chunks * steps - 1)
-    def _():
-        final = chunks * steps - 1
-        reach = delay * (blocks - 1)
-        open_at = [max(1, (owner + 1) * steps - 1 + reach - final) for owner in range(chunks)]
-
-        def slot(i, carry):
-            for owner in range(chunks):
-                if (owner + 1) * steps - 1 + reach + pieces - 1 > final:
-                    relays(final + i, owner)
-            for owner in range(chunks):
-                k = i - open_at[owner]
-
-                @pl.when((k >= 0) & (k < pieces))
-                def _():
-                    def one(q, carry):
-                        trace_problem(
-                            (owner * pieces + k) * size + q, modes, up_got, down_got, rims,
-                            single, tables, pay, here=here,
-                        )
-                        return carry
-
-                    lax.fori_loop(0, size, one, 0)
-
-            return carry
-
-        lax.fori_loop(1, max(open_at) + pieces, slot, 0)
-        ups = pltpu.make_async_copy(up_got, up_all, moved.at[chunks])
-        downs = pltpu.make_async_copy(down_got, down_all, moved.at[chunks + 1])
-        ups.start()
-        downs.start()
-        chain.finish(chunks * pieces)
-        ups.wait()
-        downs.wait()
-        for c in range(chunks):
-            move(c).wait()
 
 
 def sweep_problem(b, modes, flux, up1, up2, down1, down2, single, tables, wave, *, here, levels):
@@ -462,168 +320,361 @@
     return jnp.concatenate([ref[i, kind] for i in range(devices)], axis=0)
 
 
+SCRATCH = (
+    "mult", "aux", "start", "end", "col", "row", "home", "single", "ahead", "after", "mix",
+    "mix_back", "ring",
+    "prev", "body", "tail", "rims", "modes", "pay", "recv", "back", "came", "flux",
+    "own_up1", "own_down1", "got_up1", "got_down1", "out_up1", "out_down1",
+    "own_up2", "own_down2", "got_up2", "got_down2", "out_up2", "out_down2",
+    "streamed", "fetched", "moved",
+    "sent_up1", "sent_down1", "came_up1", "came_down1",
+    "sent_up2", "sent_down2", "came_up2", "came_down2",
+    "sent1", "came1", "sent2", "came2",
+)
+
+
+def loop(low, high, action, unroll=1):
+    def one(i, carry):
+        action(i)
+        return carry
+
+    if not (isinstance(low, int) and isinstance(high, int) and high <= low):
+        lax.fori_loop(low, high, one, 0, unroll=unroll)
+
+
 def solve_kernel(
-    pay, modes_all, up_all, down_all, rims, single, tables_all, mix, mix_back, ring,
-    col_table, row_back,
-    phi_all, edges,
-    recv, back, came, flux, modes, wave, tables, up1, down1,
-    up_own, down_own, up_got, down_got, up_out, down_out,
-    up_sent, up_came, down_sent, down_came, sent1, came1, sent2, came2, loaded, moved,
-    *, levels, here, blocks, group, inner, pieces, delay
+    mult_all, aux_all, start_all, end_all, col_all, row_all, home_all, single_all, ahead_all,
+    after_all, mix_all, mix_back_all, ring_all, phi_all, edges, *scratch,
+    levels, here, blocks, inner, pieces, delay, depth
 ):
-    problems, rows, cols = up1.shape
-    devices, width = pay.shape[0], pay.shape[3]
+    s = types.SimpleNamespace(**dict(zip(SCRATCH, scratch)))
+    problems, rows, cols = s.start.shape
+    devices, width = s.pay.shape[0], s.pay.shape[3]
+    chunk, per, half = problems // 2, pieces // 2, devices // 2
+    size = problems // pieces
     parts = cols // width
-    size = problems // pieces
+    reach = delay * (blocks - 1)
     me_py = lax.axis_index("py")
-    me = (lax.axis_index("grp") * inner + lax.axis_index("px")) * blocks + me_py
-    chain = Chain(
-        (up_own, up_got, up_out, up_sent, up_came),
-        (down_own, down_got, down_out, down_sent, down_came),
-        single.at[1], size, blocks,
-    )
-
-    def place(i):
+    me_space = lax.axis_index("grp") * inner + lax.axis_index("px")
+    me = me_space * blocks + me_py
+    my_half = me_space % 2
+    my_chunk = my_half * half + (me_space // 2) * blocks + me_py
+    tables, after = s.ahead, s.after
+
+    def where(flat):
+        return {
+            "grp": flat // (inner * blocks),
+            "px": flat // blocks % inner,
+            "py": flat % blocks,
+        }
+
+    def solver(c):
+        i = c % half
+        return (2 * (i // blocks) + c // half) * blocks + i % blocks
+
+    def chain(n):
+        part = lambda name: getattr(s, name % n)
+        return Chain(
+            *((part("own_%s%%d" % way), part("got_%s%%d" % way), part("out_%s%%d" % way),
+               part("sent_%s%%d" % way), part("came_%s%%d" % way)) for way in ("up", "down")),
+            s.single.at[1], size, blocks,
+        )
+
+    chain1, chain2 = chain(1), chain(2)
+
+    def relays(which, i, owner):
+        for way in range(2):
+            k = i - delay * which.far[way]
+            which.relay(way, owner * per + k, owner * per, (owner + 1) * per)
+
+    def stream(g):
+        c, t, at = g // here, g % here, g % depth
+        cut = pl.ds(c * chunk, chunk)
+        return [
+            pltpu.make_async_copy(mult_all.at[:, t, cut], s.mult.at[at], s.streamed.at[0, at]),
+            pltpu.make_async_copy(aux_all.at[:, t, cut], s.aux.at[at], s.streamed.at[1, at]),
+        ]
+
+    pairs = [
+        (start_all, s.start), (end_all, s.end), (col_all, s.col), (row_all, s.row),
+        (single_all, s.single), (ahead_all.at[me_py], s.ahead), (after_all.at[me_py], s.after),
+        (mix_all, s.mix), (mix_back_all, s.mix_back), (ring_all.at[:, my_chunk % parts], s.ring),
+        (home_all, s.home),
+    ]
+    fetches = [pltpu.make_async_copy(x, y, s.fetched.at[i]) for i, (x, y) in enumerate(pairs)]
+    early = 6
+    for g in range(min(depth, 2 * here)):
+        for copy in stream(g):
+            copy.start()
+        if g == 0:
+            for fetch in fetches[:early]:
+                fetch.start()
+    for fetch in fetches[early:]:
+        fetch.start()
+    barrier = pltpu.get_barrier_semaphore()
+
+    def hail(i):
+        pl.semaphore_signal(
+            barrier, inc=1, device_id=where((me + i) % devices), device_id_type=MESH
+        )
+
+    loop(1, devices, hail)
+    chain1.clear()
+    chain2.clear()
+    for fetch in fetches[:early]:
+        fetch.wait()
+    row = lax.broadcasted_iota(jnp.int32, (rows, cols), 0)
+
+    def transform(c, t):
+        base = c * chunk
+        spread = times_table(s.body[...].reshape(chunk * rows, cols), s.col)
+        s.modes[t, base : base + chunk] = over_rows(s.row, spread.reshape(chunk, rows, cols))
+        ratio, low, falling = s.single[0], tables[t], tables[2 * (here + 1) + t]
+
+        def add(b):
+            value = s.modes[t, b]
+            s.own_up1[b] = ratio * s.own_up1[b] + low * value
+            s.own_down1[b] = s.own_down1[b] + falling * value
+
+        loop(base, base + chunk, add, unroll=4)
+
+    def source(c, t):
+        g = c * here + t
+        at = g % depth
+        level = me_py * here + t
+        for copy in stream(g):
+            copy.wait()
+        keep = jnp.where(level == levels - 1, 0.0, 1.0)
+        begin = jnp.where(level == 0, -1.0 / PENALTY, 0.0)
+        finish = jnp.where(level == levels - 1, 1.0 / PENALTY, 0.0)
+
+        def one(b):
+            along = s.aux[at, 1, b] - s.mult[at, 1, b] / PENALTY
+            s.tail[b, pl.ds(t, 1), :] = along[rows - 1 :, :]
+            beside = jnp.where(row == 0, 0.0, pltpu.roll(along, 1, 0))
+            along = jnp.where(row == rows - 1, 0.0, along)
+            second = s.aux[at, 2, b] - s.mult[at, 2, b] / PENALTY
+            across = pltpu.roll(second, 1, 1) - second
+            now = (s.aux[at, 0, b] - s.mult[at, 0, b] / PENALTY) * keep
+            boundary = begin * s.start[c * chunk + b] + finish * s.end[c * chunk + b]
+            s.body[b] = s.prev[b] - now + beside - along + across + boundary
+            s.prev[b] = now
+
+        loop(0, chunk, one, unroll=4)
+
+        @pl.when(g + depth < 2 * here)
+        def _():
+            for copy in stream(g + depth):
+                copy.start()
+
+        transform(c, t)
+        if c == 1:
+            relays(chain1, t + 1, 0)
+
+    for c in range(2):
+        cut = slice(c * chunk, c * chunk + chunk)
+        s.prev[...] = jnp.zeros_like(s.prev)
+        s.tail[...] = jnp.zeros_like(s.tail)
+        s.own_up1[cut] = jnp.zeros((chunk, rows, cols), f32)
+        s.own_down1[cut] = jnp.zeros((chunk, rows, cols), f32)
+        loop(0, here, functools.partial(source, c))
+        s.body[...] = s.prev[...]
+        transform(c, here)
+        held = s.tail.shape[1]
+        if c == 0:
+            pl.semaphore_wait(barrier, devices - 1)
+        loop(c * per, (c + 1) * per, chain1.begin)
+        if c == 1:
+            relays(chain1, here + 1, 0)
+        flat = s.tail[...].reshape(chunk * held, cols)
+        s.rims[cut] = times_table(flat, s.col).reshape(chunk, held, cols)
+
+    def ask(c):
+        other = solver(c)
+
+        @pl.when(other == me)
+        def _():
+            s.recv[me] = s.pay[c]
+
+        @pl.when(other != me)
+        def _():
+            pltpu.make_async_remote_copy(
+                src_ref=s.pay.at[c], dst_ref=s.recv.at[me], send_sem=s.sent1.at[c],
+                recv_sem=s.came1.at[me], device_id=where(other), device_id_type=MESH,
+            ).start()
+
+    def trace(k):
+        def one(b):
+            trace_problem(
+                b, s.modes, s.got_up1, s.got_down1, s.rims, s.single, tables, s.pay, here=here
+            )
+            for n in range(parts):
+                ask(b * parts + n)
+
+        loop(k * size, k * size + size, one)
+
+    def answer(i):
         other = (me + i) % devices
-        where = {
-            "grp": other // (inner * blocks),
-            "px": other // blocks % inner,
-            "py": other % blocks,
-        }
-        return other, where
-
-    loads = [
-        pltpu.make_async_copy(modes_all, modes, loaded.at[0]),
-        pltpu.make_async_copy(up_all, up1, loaded.at[1]),
-        pltpu.make_async_copy(down_all, down1, loaded.at[2]),
-        pltpu.make_async_copy(tables_all.at[me_py], tables, loaded.at[3]),
-    ]
-
-    barrier = pltpu.get_barrier_semaphore()
-
-    def hail(i, carry):
-        _, where = place(i)
-        pl.semaphore_signal(barrier, inc=1, device_id=where, device_id_type=MESH)
-        return carry
-
-    lax.fori_loop(1, devices, hail, 0)
-    for load in loads:
-        load.start()
-    chain.clear()
-    pl.semaphore_wait(barrier, devices - 1)
-
-    def exchange(source, target, sent, arrived, i):
-        other, where = place(i)
         return pltpu.make_async_remote_copy(
-            src_ref=source.at[other],
-            dst_ref=target.at[me],
-            send_sem=sent.at[i],
-            recv_sem=arrived.at[i],
-            device_id=where,
-            device_id_type=MESH,
+            src_ref=s.back.at[other], dst_ref=s.came.at[my_chunk], send_sem=s.sent2.at[i],
+            recv_sem=s.came2.at[my_chunk], device_id=where(other), device_id_type=MESH,
         )
 
-    def every(action):
-        def one(i, carry):
-            action(i)
-            return carry
-
-        lax.fori_loop(1, devices, one, 0)
-
-    first = lambda i: exchange(pay, recv, sent1, came1, i)
-    second = lambda i: exchange(back, came, sent2, came2, i)
-    every(lambda i: first(i).start())
-    recv[me] = pay[me]
-    every(lambda i: first(i).wait_recv())
-
-    total = devices * here
-    lane = lax.broadcasted_iota(jnp.int32, (total, width), 1)
-    slot_id = me % parts
-    jump = pltpu.roll(flat_rows(recv, 0, here), total - levels, 0) - flat_rows(recv, 1, here)
-    flat = flat_rows(recv, 2, here)
-    beyond = pltpu.roll(pltpu.roll(flat, here, 0), width - 1, 1)
-    whole = jnp.where(lane == 0, flat + beyond, 0.0)
-    jump_flat = pltpu.roll(whole, total - levels, 0) - whole
-    solved = precise(mix[...], jump) * ring[0, slot_id]
-    solved = solved + precise(mix[...], jump_flat) * ring[1, slot_id]
-    mine = precise(mix_back[...], solved)
-    other = pltpu.roll(mine, levels, 0)
-    if here % 8 == 0:
-        back[:, 0] = mine.reshape(devices, here, width)
-        back[:, 1] = other.reshape(devices, here, width)
-    else:
-        for i in range(devices):
-            back[i, 0] = mine[i * here : (i + 1) * here]
-            back[i, 1] = other[i * here : (i + 1) * here]
-    every(lambda i: second(i).start())
-    came[me] = back[me]
-    every(lambda i: second(i).wait_recv())
-    for i in range(devices):
-        b, n = i // parts, i % parts
-        for kind in range(2):
-            flux[b, kind * here : (kind + 1) * here, n * width : (n + 1) * width] = came[i, kind]
-    for load in loads:
-        load.wait()
-
-    reach = delay * (blocks - 1)
+    def solve_ring(h):
+        @pl.when(my_half == h)
+        def _():
+            def arrive(i):
+                other = (me + i) % devices
+                pltpu.make_async_remote_copy(
+                    src_ref=s.pay.at[0], dst_ref=s.recv.at[other], send_sem=s.sent1.at[0],
+                    recv_sem=s.came1.at[other], device_id=where(other), device_id_type=MESH,
+                ).wait_recv()
+
+            loop(1, devices, arrive)
+            total = devices * here
+            lane = lax.broadcasted_iota(jnp.int32, (total, width), 1)
+            ahead = total - levels
+            jump = pltpu.roll(flat_rows(s.recv, 0, here), ahead, 0) - flat_rows(s.recv, 1, here)
+            flat = flat_rows(s.recv, 2, here)
+            beyond = pltpu.roll(pltpu.roll(flat, here, 0), width - 1, 1)
+            whole = jnp.where(lane == 0, flat + beyond, 0.0)
+            jump_flat = pltpu.roll(whole, ahead, 0) - whole
+            solved = precise(s.mix[...], jump) * s.ring[0]
+            solved = solved + precise(s.mix[...], jump_flat) * s.ring[1]
+            mine = precise(s.mix_back[...], solved)
+            other = pltpu.roll(mine, levels, 0)
+            if here % 8 == 0:
+                s.back[:, 0] = mine.reshape(devices, here, width)
+                s.back[:, 1] = other.reshape(devices, here, width)
+            else:
+                for i in range(devices):
+                    s.back[i, 0] = mine[i * here : (i + 1) * here]
+                    s.back[i, 1] = other[i * here : (i + 1) * here]
+            loop(1, devices, lambda i: answer(i).start())
+            s.came[my_chunk] = s.back[me]
+
+    def fluxes(h):
+        def arrive(c):
+            other = solver(c)
+
+            @pl.when(other != me)
+            def _():
+                pltpu.make_async_remote_copy(
+                    src_ref=s.back.at[0], dst_ref=s.came.at[c], send_sem=s.sent2.at[0],
+                    recv_sem=s.came2.at[c], device_id=where(other), device_id_type=MESH,
+                ).wait_recv()
+
+        loop(h * half, (h + 1) * half, arrive)
+        for c in range(h * half, (h + 1) * half):
+            b, n = c // parts, c % parts
+            for kind in range(2):
+                s.flux[b, kind * here : (kind + 1) * here, n * width : (n + 1) * width] = (
+                    s.came[c, kind]
+                )
+
+        def own(k):
+            loop(k * size, k * size + size, lambda b: flux_problem(
+                b, s.flux, after, s.own_up2, s.own_down2, here=here))
+            chain2.begin(k)
+
+        loop(h * per, (h + 1) * per, own)
 
     def send_out(k):
         cut = pl.ds(k * size, size)
         return pltpu.make_async_copy(
-            wave.at[pl.ds(0, here), cut], phi_all.at[pl.ds(0, here), cut], moved.at[k]
+            s.modes.at[pl.ds(0, here), cut], phi_all.at[pl.ds(0, here), cut], s.moved.at[k]
         )
 
-    def slot(i, carry):
-        @pl.when(i < pieces)
-        def _():
-            def one(q, carry):
-                flux_problem(i * size + q, flux, tables, up_own, down_own, here=here)
-                return carry
-
-            lax.fori_loop(0, size, one, 0)
-            chain.begin(i)
-
-        for way in range(2):
-            chain.relay(way, i - delay * chain.far[way], 0, pieces)
-
-        k = i - reach
-
-        @pl.when(k >= 0)
-        def _():
-            def one(q, carry):
-                sweep_problem(
-                    k * size + q, modes, flux, up1, up_got, down1, down_got, single, tables,
-                    wave, here=here, levels=levels,
-                )
-                return carry
-
-            lax.fori_loop(0, size, one, 0)
-            cut = pl.ds(k * size, size)
-            part = over_rows(row_back, wave[0:here, cut].reshape(here * size, rows, cols))
-            part = times_table(part.reshape(here * size * rows, cols), col_table)
-            wave[0:here, cut] = part.reshape(here, size, rows, cols)
-            send_out(k).start()
-
-        return carry
-
-    lax.fori_loop(0, pieces + reach, slot, 0)
-    last = over_rows(row_back, wave[here])
-    last = times_table(last.reshape(problems * rows, cols), col_table)
-    wave[here] = last.reshape(problems, rows, cols)
-    tip = pltpu.make_async_copy(wave.at[here], phi_all.at[here], moved.at[pieces])
-    tip.start()
-    if here % 8 == 0:
-        rim = (flux[:, 0:here, :] + rims[:, 0:here, :]).reshape(problems * here, cols)
-        edges[...] = times_table(rim, col_table).reshape(problems, here, cols)
-    else:
-        for b in range(problems):
-            edges[b] = times_table(flux[b, 0:here, :] + rims[b, 0:here, :], col_table)
-    chain.finish(pieces)
-    every(lambda i: first(i).wait_send())
-    every(lambda i: second(i).wait_send())
-    for k in range(pieces):
-        send_out(k).wait()
-    tip.wait()
+    def send_tip(h):
+        cut = pl.ds(h * chunk, chunk)
+        return pltpu.make_async_copy(
+            s.modes.at[here, cut], phi_all.at[here, cut], s.moved.at[pieces + h]
+        )
+
+    def sweep(k):
+        loop(k * size, k * size + size, lambda b: sweep_problem(
+            b, s.modes, s.flux, s.got_up1, s.got_up2, s.got_down1, s.got_down2, s.single, after,
+            s.modes, here=here, levels=levels))
+        cut = pl.ds(k * size, size)
+        part = over_rows(s.home, s.modes[0:here, cut].reshape(here * size, rows, cols))
+        part = times_table(part.reshape(here * size * rows, cols), s.col)
+        s.modes[0:here, cut] = part.reshape(here, size, rows, cols)
+        send_out(k).start()
+
+    def tip(h):
+        cut = slice(h * chunk, h * chunk + chunk)
+        last = over_rows(s.home, s.modes[here, cut])
+        last = times_table(last.reshape(chunk * rows, cols), s.col)
+        s.modes[here, cut] = last.reshape(chunk, rows, cols)
+        send_tip(h).start()
+        for b in range(h * chunk, h * chunk + chunk):
+            edges[b] = times_table(s.flux[b, 0:here, :] + s.rims[b, 0:here, :], s.col)
+
+    filled = max(per, reach - 1)
+
+    def drain1(i):
+        relays(chain1, i, 1)
+
+        @pl.when(i <= per)
+        def _():
+            trace(i - 1)
+
+    def drain2(k):
+        @pl.when(reach + k > filled)
+        def _():
+            relays(chain1, reach + k, 1)
+
+        trace(per + k)
+
+    loop(here + 2, reach + per, lambda i: relays(chain1, i, 0))
+    loop(1, filled + 1, drain1)
+    for fetch in fetches[early:]:
+        fetch.wait()
+    solve_ring(0)
+    loop(0, per, drain2)
+    fluxes(0)
+    loop(1, 3, lambda i: relays(chain2, i, 0))
+    solve_ring(1)
+    loop(3, reach + per, lambda i: relays(chain2, i, 0))
+    fluxes(1)
+
+    def drain3(i):
+        relays(chain2, i, 1)
+
+        @pl.when(i <= per)
+        def _():
+            sweep(i - 1)
+
+    def drain4(k):
+        @pl.when(reach + k > filled)
+        def _():
+            relays(chain2, reach + k, 1)
+
+        sweep(per + k)
+
+    loop(1, filled + 1, drain3)
+    tip(0)
+    loop(0, per, drain4)
+    tip(1)
+
+    chain1.finish(pieces)
+    chain2.finish(pieces)
+
+    def asked(c):
+        other = solver(c)
+
+        @pl.when(other != me)
+        def _():
+            pltpu.make_async_remote_copy(
+                src_ref=s.pay.at[c], dst_ref=s.recv.at[me], send_sem=s.sent1.at[c],
+                recv_sem=s.came1.at[me], device_id=where(other), device_id_type=MESH,
+            ).wait_send()
+
+    loop(0, devices, asked)
+    loop(1, devices, lambda i: answer(i).wait_send())
+    loop(0, pieces, lambda k: send_out(k).wait())
+    for h in range(2):
+        send_tip(h).wait()
 
 
 def project_kernel(phi, following, edges, mult, next_mult, next_aux, *, levels):
@@ -693,71 +744,50 @@
     held = -(-here // 8) * 8
     width = problems * cols // devices
     parts = cols // width
-    shape = lambda *s: jax.ShapeDtypeStruct(s, f32)
-    vector = lambda *s: pltpu.VMEM(s, f32)
+    total = devices * here
+    delay, depth = 2, 4
+    chunk = problems // 2
+    pieces = 2 * math.gcd(chunk, 4)
+    size = problems // pieces
+    fit = max(1, 256 // rows)
+    shape = lambda *dims: jax.ShapeDtypeStruct(dims, f32)
+    vector = lambda *dims: pltpu.VMEM(dims, f32)
     anywhere = pl.BlockSpec(memory_space=pl.ANY)
-    vmem = pl.BlockSpec(memory_space=pltpu.VMEM)
-    dma = lambda n: pltpu.SemaphoreType.DMA((n,))
-    delay = 2
-
-    chunks = 2
-    chunk = problems // chunks
-    pieces = math.gcd(chunk, 4)
-    bunch = math.gcd(chunk, max(1, 256 // rows))
-    col_table = jnp.asarray(halves(hartley(cols)))
-    row_table = jnp.asarray(halves(np.kron(np.eye(bunch), cosines(rows))))
+    dma = lambda *dims: pltpu.SemaphoreType.DMA(dims)
+
+    col_table = halves(hartley(cols))
+    row_table = halves(np.kron(np.eye(math.gcd(chunk, fit)), cosines(rows)))
+    row_back = halves(np.kron(np.eye(math.gcd(math.gcd(size * here, chunk), fit)), cosines(rows).T))
     single, ahead, after = slab_tables(rows, cols, here, blocks)
-    single, ahead, after = jnp.asarray(single), jnp.asarray(ahead), jnp.asarray(after)
-
-    plane = (problems, rows, cols)
-    level_block = pl.BlockSpec(
-        (3, 1, chunk, rows, cols), lambda c, t: (0, jnp.minimum(t, here - 1), c, 0, 0)
-    )
-    density_block = pl.BlockSpec((chunk, rows, cols), lambda c, t: (c, 0, 0))
-    modes, up1, down1, rims, pay = pl.pallas_call(
-        functools.partial(source_kernel, levels=levels, here=here, blocks=blocks, chunks=chunks,
-                          pieces=pieces, delay=delay),
-        out_shape=(shape(here + 1, *plane), shape(*plane), shape(*plane),
-                   shape(problems, held, cols), shape(devices, 3, here, width)),
-        grid=(chunks, here + 1),
-        in_specs=[level_block, level_block, density_block, density_block,
-                  whole_block(col_table.shape), whole_block(row_table.shape),
-                  whole_block(single.shape), anywhere],
-        out_specs=(anywhere, anywhere, anywhere, whole_block((problems, held, cols)),
-                   whole_block((devices, 3, here, width))),
-        scratch_shapes=[vector(here + 1, *plane), vector(chunk, rows, cols),
-                        vector(chunk, rows, cols), vector(chunk, held, cols),
-                        vector(*ahead.shape[1:])] + [vector(*plane)] * 6
-        + [dma(chunks * pieces)] * 4 + [dma(chunks + 2), pltpu.SemaphoreType.DMA],
-        compiler_params=params(0),
-        name="source",
-    )(multiplier, auxiliary, density_start, density_end, col_table, row_table, single, ahead)
-
     mix, inverse, extra = ring_tables(rows, cols, group, levels)
-    total = devices * here
     wide = np.zeros((total, cols), np.float32)
     wide[:, :1] = extra
     ring = np.stack([inverse, wide]).reshape(2, total, parts, width).transpose(0, 2, 1, 3).copy()
-    pieces = math.gcd(problems, 8)
-    size = problems // pieces
-    bunch = math.gcd(math.gcd(size * here, problems), max(1, 256 // rows))
-    row_back = jnp.asarray(halves(np.kron(np.eye(bunch), cosines(rows).T)))
+    tables = [col_table, row_table, row_back, single, ahead, after, mix, mix.T.copy(), ring]
+
+    plane = (problems, rows, cols)
+    part = (chunk, rows, cols)
+    table = lambda x: pltpu.VMEM(x.shape, x.dtype)
+    scratch = [
+        vector(depth, 3, *part), vector(depth, 3, *part), vector(*plane), vector(*plane),
+        table(col_table), table(row_table), table(row_back), table(single), table(ahead[0]),
+        table(after[0]), table(mix), table(mix), table(ring[:, 0]),
+        vector(*part), vector(*part), vector(chunk, held, cols), vector(problems, held, cols),
+        vector(here + 1, *plane), vector(devices, 3, here, width),
+        vector(devices, 3, here, width), vector(devices, 2, here, width),
+        vector(devices, 2, here, width), vector(problems, 2 * here, cols),
+    ] + [vector(*plane)] * 12 + [dma(2, depth), dma(11), dma(pieces + 2)]
+    scratch += [dma(pieces)] * 8 + [dma(devices)] * 4
     phi, edges = pl.pallas_call(
-        functools.partial(solve_kernel, levels=levels, here=here, blocks=blocks, group=group,
-                          inner=inner, pieces=pieces, delay=delay),
+        functools.partial(solve_kernel, levels=levels, here=here, blocks=blocks, inner=inner,
+                          pieces=pieces, delay=delay, depth=depth),
         out_shape=(shape(here + 1, *plane), shape(problems, here, cols)),
-        in_specs=[vmem, anywhere, anywhere, anywhere, vmem, vmem, anywhere, vmem, vmem, vmem,
-                  vmem, vmem],
-        out_specs=(anywhere, vmem),
-        scratch_shapes=[vector(devices, 3, here, width), vector(devices, 2, here, width),
-                        vector(devices, 2, here, width), vector(problems, 2 * here, cols),
-                        vector(here + 1, *plane), vector(here + 1, *plane),
-                        vector(*after.shape[1:])] + [vector(*plane)] * 8
-        + [dma(pieces)] * 4 + [dma(devices)] * 4 + [dma(4), dma(pieces + 1)],
-        compiler_params=params(1),
+        in_specs=[anywhere] * 13,
+        out_specs=(anywhere, pl.BlockSpec(memory_space=pltpu.VMEM)),
+        scratch_shapes=scratch,
+        compiler_params=params(0),
         name="solve",
-    )(pay, modes, up1, down1, rims, single, after, jnp.asarray(mix), jnp.asarray(mix.T.copy()),
-      jnp.asarray(ring), col_table, row_back)
+    )(multiplier, auxiliary, density_start, density_end, *(jnp.asarray(x) for x in tables))
 
     out_shape = shape(*multiplier.shape)
     level_block = pl.BlockSpec((3, 1, *plane), lambda t: (0, t, 0, 0, 0))

time: 126 us -> 113 us (0.90)
  Pallas kernels: 125 us -> 112 us
    pallas_call x1 -> x0, Pallas kernels: 48 us -> none  [local(): pl.pallas_call(functools.partial(source_kernel, levels=levels, here=here,...]
    pallas_call x1, Pallas kernels: 52.7 us -> 87.8 us  [local(): pl.pallas_call(functools.partial(solve_kernel, levels=levels, here=here,...]
where the time goes in v3:
time: 113 us; the launch traced here: 112 us
  Pallas kernels  112 us (99%)
    pallas_call x1, Pallas kernels, local(): pl.pallas_call(functools.partial(solve_kernel, levels=levels, here=here,...  87.8 us
    pallas_call x1, Pallas kernels, local(): pl.pallas_call(functools.partial(project_kernel, levels=levels), out_shap...  23.9 us

profile of v3, /device:TPU:0, one launch (start us, length us, event | category | flops | bytes accessed | tf_op | source)
XLA Modules:
  0.0 112.3 jit_solution(15490147250637419373)
XLA Ops:
  0.6 87.8 %solve.1 = (f32[9,16,32,256]{3,2,1,0:T(8,128)}, f32[16,8,256]{2,1,0:T(8,128)}) custom-call(f32[3,8,16,32,256]{4,3,2,1,0:T(8,128)} %mult.1, f32[3,8,16,32,256]{4,3,2,1,0:T(8,128)} %aux_all.1, f32[16,32,256]{2,1,0:T(8,128)} %start_all.1, f32[16,32,256]{2,1,0:T(8,128)} %end_all.1, bf16[2,256,256]{2,1,0:T(8,128)(2,1)} %constant.18.clone.col_all, ...), custom_call_target="tpu_custom_call" | custom-call | tf_op jit(solution)/shard_map/solve/pallas_call | solution.py:781
  88.4 23.9 %project.1 = (f32[3,8,16,32,256]{4,3,2,1,0:T(8,128)}, f32[3,8,16,32,256]{4,3,2,1,0:T(8,128)}) custom-call(f32[9,16,32,256]{3,2,1,0:T(8,128)} %get-tuple-element.4.phi.following, f32[9,16,32,256]{3,2,1,0:T(8,128)} %get-tuple-element.4.phi.following, f32[16,8,256]{2,1,0:T(8,128)} %get-tuple-element.5.edges, f32[3,8,16,32,256]{4,3,2,1,0:T(8,128)} %mult.1), custom_call_target="tpu_custom_call" | custom-call | tf_op jit(solution)/shard_map/project/pallas_call | solution.py:796

commit v4 on v3

--- a/solution.py
+++ b/solution.py
@@ -323,13 +323,13 @@
 SCRATCH = (
     "mult", "aux", "start", "end", "col", "row", "home", "single", "ahead", "after", "mix",
     "mix_back", "ring",
-    "prev", "body", "tail", "rims", "modes", "pay", "recv", "back", "came", "flux",
+    "prev", "body", "spread", "tail", "rims", "modes", "pay", "recv", "back", "came", "flux",
     "own_up1", "own_down1", "got_up1", "got_down1", "out_up1", "out_down1",
     "own_up2", "own_down2", "got_up2", "got_down2", "out_up2", "out_down2",
     "streamed", "fetched", "moved",
     "sent_up1", "sent_down1", "came_up1", "came_down1",
     "sent_up2", "sent_down2", "came_up2", "came_down2",
-    "sent1", "came1", "sent2", "came2",
+    "sent1", "came1", "sent2", "came2", "sent3", "came3",
 )
 
 
@@ -421,22 +421,27 @@
     loop(1, devices, hail)
     chain1.clear()
     chain2.clear()
+
+    @pl.when(my_chunk % parts != 0)
+    def _():
+        s.recv[:, 2] = jnp.zeros((devices, here, width), f32)
+
     for fetch in fetches[:early]:
         fetch.wait()
     row = lax.broadcasted_iota(jnp.int32, (rows, cols), 0)
 
-    def transform(c, t):
+    def across_rows(c, v):
         base = c * chunk
-        spread = times_table(s.body[...].reshape(chunk * rows, cols), s.col)
-        s.modes[t, base : base + chunk] = over_rows(s.row, spread.reshape(chunk, rows, cols))
-        ratio, low, falling = s.single[0], tables[t], tables[2 * (here + 1) + t]
-
-        def add(b):
-            value = s.modes[t, b]
+        s.modes[v, base : base + chunk] = over_rows(s.row, s.spread[...])
+        ratio, low, falling = s.single[0], tables[v], tables[2 * (here + 1) + v]
+        for b in range(base, base + chunk):
+            value = s.modes[v, b]
             s.own_up1[b] = ratio * s.own_up1[b] + low * value
             s.own_down1[b] = s.own_down1[b] + falling * value
 
-        loop(base, base + chunk, add, unroll=4)
+    def across_cols(values):
+        flat = values[...].reshape(chunk * rows, cols)
+        s.spread[...] = times_table(flat, s.col).reshape(chunk, rows, cols)
 
     def source(c, t):
         g = c * here + t
@@ -444,30 +449,28 @@
         level = me_py * here + t
         for copy in stream(g):
             copy.wait()
+        across_rows(c, jnp.maximum(t - 1, 0))
         keep = jnp.where(level == levels - 1, 0.0, 1.0)
         begin = jnp.where(level == 0, -1.0 / PENALTY, 0.0)
         finish = jnp.where(level == levels - 1, 1.0 / PENALTY, 0.0)
-
-        def one(b):
+        for b in range(chunk):
             along = s.aux[at, 1, b] - s.mult[at, 1, b] / PENALTY
             s.tail[b, pl.ds(t, 1), :] = along[rows - 1 :, :]
             beside = jnp.where(row == 0, 0.0, pltpu.roll(along, 1, 0))
             along = jnp.where(row == rows - 1, 0.0, along)
             second = s.aux[at, 2, b] - s.mult[at, 2, b] / PENALTY
-            across = pltpu.roll(second, 1, 1) - second
+            side = pltpu.roll(second, 1, 1) - second
             now = (s.aux[at, 0, b] - s.mult[at, 0, b] / PENALTY) * keep
             boundary = begin * s.start[c * chunk + b] + finish * s.end[c * chunk + b]
-            s.body[b] = s.prev[b] - now + beside - along + across + boundary
+            s.body[b] = s.prev[b] - now + beside - along + side + boundary
             s.prev[b] = now
-
-        loop(0, chunk, one, unroll=4)
+        across_cols(s.body)
 
         @pl.when(g + depth < 2 * here)
         def _():
             for copy in stream(g + depth):
                 copy.start()
 
-        transform(c, t)
         if c == 1:
             relays(chain1, t + 1, 0)
 
@@ -475,11 +478,13 @@
         cut = slice(c * chunk, c * chunk + chunk)
         s.prev[...] = jnp.zeros_like(s.prev)
         s.tail[...] = jnp.zeros_like(s.tail)
+        s.spread[...] = jnp.zeros_like(s.spread)
         s.own_up1[cut] = jnp.zeros((chunk, rows, cols), f32)
         s.own_down1[cut] = jnp.zeros((chunk, rows, cols), f32)
         loop(0, here, functools.partial(source, c))
-        s.body[...] = s.prev[...]
-        transform(c, here)
+        across_rows(c, here - 1)
+        across_cols(s.prev)
+        across_rows(c, here)
         held = s.tail.shape[1]
         if c == 0:
             pl.semaphore_wait(barrier, devices - 1)
@@ -489,7 +494,16 @@
         flat = s.tail[...].reshape(chunk * held, cols)
         s.rims[cut] = times_table(flat, s.col).reshape(chunk, held, cols)
 
-    def ask(c):
+    def question(c, flat, source, target):
+        kinds = pl.ds(2, 1) if flat else pl.ds(0, 2)
+        return pltpu.make_async_remote_copy(
+            src_ref=s.pay.at[c, kinds], dst_ref=s.recv.at[source, kinds],
+            send_sem=(s.sent3 if flat else s.sent1).at[c],
+            recv_sem=(s.came3 if flat else s.came1).at[source],
+            device_id=where(target), device_id_type=MESH,
+        )
+
+    def ask(c, flat):
         other = solver(c)
 
         @pl.when(other == me)
@@ -498,10 +512,9 @@
 
         @pl.when(other != me)
         def _():
-            pltpu.make_async_remote_copy(
-                src_ref=s.pay.at[c], dst_ref=s.recv.at[me], send_sem=s.sent1.at[c],
-                recv_sem=s.came1.at[me], device_id=where(other), device_id_type=MESH,
-            ).start()
+            question(c, False, me, other).start()
+            if flat:
+                question(c, True, me, other).start()
 
     def trace(k):
         def one(b):
@@ -509,7 +522,7 @@
                 b, s.modes, s.got_up1, s.got_down1, s.rims, s.single, tables, s.pay, here=here
             )
             for n in range(parts):
-                ask(b * parts + n)
+                ask(b * parts + n, n == 0)
 
         loop(k * size, k * size + size, one)
 
@@ -525,10 +538,11 @@
         def _():
             def arrive(i):
                 other = (me + i) % devices
-                pltpu.make_async_remote_copy(
-                    src_ref=s.pay.at[0], dst_ref=s.recv.at[other], send_sem=s.sent1.at[0],
-                    recv_sem=s.came1.at[other], device_id=where(other), device_id_type=MESH,
-                ).wait_recv()
+                question(0, False, other, other).wait_recv()
+
+                @pl.when(my_chunk % parts == 0)
+                def _():
+                    question(0, True, other, other).wait_recv()
 
             loop(1, devices, arrive)
             total = devices * here
@@ -652,42 +666,49 @@
 
         sweep(per + k)
 
+    def asked(c):
+        other = solver(c)
+
+        @pl.when(other != me)
+        def _():
+            question(c, False, me, other).wait_send()
+
+            @pl.when(c % parts == 0)
+            def _():
+                question(c, True, me, other).wait_send()
+
     loop(1, filled + 1, drain3)
     tip(0)
+    chain1.finish(pieces)
+    loop(0, devices, asked)
+    loop(1, devices, lambda i: answer(i).wait_send())
     loop(0, per, drain4)
     tip(1)
 
-    chain1.finish(pieces)
     chain2.finish(pieces)
-
-    def asked(c):
-        other = solver(c)
-
-        @pl.when(other != me)
-        def _():
-            pltpu.make_async_remote_copy(
-                src_ref=s.pay.at[c], dst_ref=s.recv.at[me], send_sem=s.sent1.at[c],
-                recv_sem=s.came1.at[me], device_id=where(other), device_id_type=MESH,
-            ).wait_send()
-
-    loop(0, devices, asked)
-    loop(1, devices, lambda i: answer(i).wait_send())
     loop(0, pieces, lambda k: send_out(k).wait())
     for h in range(2):
         send_tip(h).wait()
 
 
-def project_kernel(phi, following, edges, mult, next_mult, next_aux, *, levels):
+def project_kernel(first, following, edges, mult, next_mult, next_aux, phi, *, levels):
     t = pl.program_id(0)
     here = pl.num_programs(0)
-    _, problems, rows, cols = phi.shape
+    _, problems, rows, cols = first.shape
+
+    @pl.when(t == 0)
+    def _():
+        phi[...] = first[0]
+
     moving = jnp.where(lax.axis_index("py") * here + t == levels - 1, 0.0, 1.0)
     row = lax.broadcasted_iota(jnp.int32, (rows, cols), 0)
 
     def one(b, carry):
-        here_phi = phi[0, b]
+        here_phi = phi[b]
+        next_phi = following[0, b]
+        phi[b] = next_phi
         rim = jnp.broadcast_to(edges[b, pl.ds(t, 1), :], (rows, cols))
-        grad_time = (following[0, b] - here_phi) * moving
+        grad_time = (next_phi - here_phi) * moving
         grad_first = jnp.where(
             row == rows - 1, rim, pltpu.roll(here_phi, rows - 1, 0) - here_phi
         )
@@ -719,7 +740,7 @@
         next_mult[2, 0, b] = mult_second + PENALTY * (grad_second - out_beside)
         return carry
 
-    lax.fori_loop(0, problems, one, 0, unroll=2)
+    lax.fori_loop(0, problems, one, 0, unroll=4)
 
 
 def params(which=None):
@@ -745,7 +766,7 @@
     width = problems * cols // devices
     parts = cols // width
     total = devices * here
-    delay, depth = 2, 4
+    delay, depth = 3, 4
     chunk = problems // 2
     pieces = 2 * math.gcd(chunk, 4)
     size = problems // pieces
@@ -772,12 +793,13 @@
         vector(depth, 3, *part), vector(depth, 3, *part), vector(*plane), vector(*plane),
         table(col_table), table(row_table), table(row_back), table(single), table(ahead[0]),
         table(after[0]), table(mix), table(mix), table(ring[:, 0]),
-        vector(*part), vector(*part), vector(chunk, held, cols), vector(problems, held, cols),
+        vector(*part), vector(*part), vector(*part), vector(chunk, held, cols),
+        vector(problems, held, cols),
         vector(here + 1, *plane), vector(devices, 3, here, width),
         vector(devices, 3, here, width), vector(devices, 2, here, width),
         vector(devices, 2, here, width), vector(problems, 2 * here, cols),
     ] + [vector(*plane)] * 12 + [dma(2, depth), dma(11), dma(pieces + 2)]
-    scratch += [dma(pieces)] * 8 + [dma(devices)] * 4
+    scratch += [dma(pieces)] * 8 + [dma(devices)] * 6
     phi, edges = pl.pallas_call(
         functools.partial(solve_kernel, levels=levels, here=here, blocks=blocks, inner=inner,
                           pieces=pieces, delay=delay, depth=depth),
@@ -791,7 +813,7 @@
 
     out_shape = shape(*multiplier.shape)
     level_block = pl.BlockSpec((3, 1, *plane), lambda t: (0, t, 0, 0, 0))
-    phi_block = pl.BlockSpec((1, *plane), lambda t: (t, 0, 0, 0))
+    phi_block = whole_block((1, *plane))
     next_block = pl.BlockSpec((1, *plane), lambda t: (t + 1, 0, 0, 0))
     return pl.pallas_call(
         functools.partial(project_kernel, levels=levels),
@@ -799,6 +821,7 @@
         grid=(here,),
         in_specs=[phi_block, next_block, whole_block(edges.shape), level_block],
         out_specs=(level_block, level_block),
+        scratch_shapes=[vector(*plane)],
         compiler_params=params(),
         name="project",
     )(phi, phi, edges, multiplier)

time: 113 us -> 100 us (0.88)
  Pallas kernels: 112 us -> 99.1 us
    pallas_call x1, Pallas kernels: 87.8 us -> 77.2 us  [local(): pl.pallas_call(functools.partial(solve_kernel, levels=levels, here=here,...]
    pallas_call x1, Pallas kernels: 23.9 us -> 21.9 us  [local(): pl.pallas_call(functools.partial(project_kernel, levels=levels), out_shap...]
where the time goes in v4:
time: 100 us; the launch traced here: 99.7 us
  Pallas kernels  99.1 us (99%)
    pallas_call x1, Pallas kernels, local(): pl.pallas_call(functools.partial(solve_kernel, levels=levels, here=here,...  77.2 us
    pallas_call x1, Pallas kernels, local(): pl.pallas_call(functools.partial(project_kernel, levels=levels), out_shap...  21.9 us

profile of v4, /device:TPU:0, one launch (start us, length us, event | category | flops | bytes accessed | tf_op | source)
XLA Modules:
  0.0 99.7 jit_solution(17283430442289545285)
XLA Ops:
  0.6 77.2 %solve.1 = (f32[9,16,32,256]{3,2,1,0:T(8,128)}, f32[16,8,256]{2,1,0:T(8,128)}) custom-call(f32[3,8,16,32,256]{4,3,2,1,0:T(8,128)} %mult.1, f32[3,8,16,32,256]{4,3,2,1,0:T(8,128)} %aux_all.1, f32[16,32,256]{2,1,0:T(8,128)} %start_all.1, f32[16,32,256]{2,1,0:T(8,128)} %end_all.1, bf16[2,256,256]{2,1,0:T(8,128)(2,1)} %constant.18.clone.col_all, ...), custom_call_target="tpu_custom_call" | custom-call | tf_op jit(solution)/shard_map/solve/pallas_call | solution.py:803
  77.8 21.9 %project.1 = (f32[3,8,16,32,256]{4,3,2,1,0:T(8,128)}, f32[3,8,16,32,256]{4,3,2,1,0:T(8,128)}) custom-call(f32[9,16,32,256]{3,2,1,0:T(8,128)} %get-tuple-element.4.first.following, f32[9,16,32,256]{3,2,1,0:T(8,128)} %get-tuple-element.4.first.following, f32[16,8,256]{2,1,0:T(8,128)} %get-tuple-element.5.edges, f32[3,8,16,32,256]{4,3,2,1,0:T(8,128)} %mult.1), custom_call_target="tpu_custom_call" | custom-call | tf_op jit(solution)/shard_map/project/pallas_call | solution.py:818

commit v5 on v4

--- a/solution.py
+++ b/solution.py
@@ -89,7 +89,7 @@
     mix = np.kron(hartley(group), cosines(levels))
     flat_rows = group * levels
     return (
-        mix.astype(np.float32),
+        mix,
         inverse.reshape(flat_rows, cols).astype(np.float32),
         extra.reshape(flat_rows, 1).astype(np.float32),
     )
@@ -112,10 +112,6 @@
 def table_times(table, x):
     high, low = split(x)
     return mm(table[0], high) + (mm(table[0], low) + mm(table[1], high))
-
-
-def precise(a, b):
-    return jnp.dot(a, b, precision=lax.Precision.HIGHEST, preferred_element_type=f32)
 
 
 def over_rows(table, x):
@@ -553,9 +549,9 @@
             beyond = pltpu.roll(pltpu.roll(flat, here, 0), width - 1, 1)
             whole = jnp.where(lane == 0, flat + beyond, 0.0)
             jump_flat = pltpu.roll(whole, ahead, 0) - whole
-            solved = precise(s.mix[...], jump) * s.ring[0]
-            solved = solved + precise(s.mix[...], jump_flat) * s.ring[1]
-            mine = precise(s.mix_back[...], solved)
+            both = table_times(s.mix, jnp.concatenate([jump, jump_flat], axis=1))
+            solved = both[:, :width] * s.ring[0] + both[:, width:] * s.ring[1]
+            mine = table_times(s.mix_back, solved)
             other = pltpu.roll(mine, levels, 0)
             if here % 8 == 0:
                 s.back[:, 0] = mine.reshape(devices, here, width)
@@ -621,8 +617,15 @@
         last = times_table(last.reshape(chunk * rows, cols), s.col)
         s.modes[here, cut] = last.reshape(chunk, rows, cols)
         send_tip(h).start()
-        for b in range(h * chunk, h * chunk + chunk):
-            edges[b] = times_table(s.flux[b, 0:here, :] + s.rims[b, 0:here, :], s.col)
+
+    def rim(h):
+        cut = slice(h * chunk, h * chunk + chunk)
+        if here % 8 == 0:
+            flat = (s.flux[cut, 0:here, :] + s.rims[cut, 0:here, :]).reshape(chunk * here, cols)
+            edges[cut] = times_table(flat, s.col).reshape(chunk, here, cols)
+        else:
+            for b in range(h * chunk, h * chunk + chunk):
+                edges[b] = times_table(s.flux[b, 0:here, :] + s.rims[b, 0:here, :], s.col)
 
     filled = max(per, reach - 1)
 
@@ -639,32 +642,6 @@
             relays(chain1, reach + k, 1)
 
         trace(per + k)
-
-    loop(here + 2, reach + per, lambda i: relays(chain1, i, 0))
-    loop(1, filled + 1, drain1)
-    for fetch in fetches[early:]:
-        fetch.wait()
-    solve_ring(0)
-    loop(0, per, drain2)
-    fluxes(0)
-    loop(1, 3, lambda i: relays(chain2, i, 0))
-    solve_ring(1)
-    loop(3, reach + per, lambda i: relays(chain2, i, 0))
-    fluxes(1)
-
-    def drain3(i):
-        relays(chain2, i, 1)
-
-        @pl.when(i <= per)
-        def _():
-            sweep(i - 1)
-
-    def drain4(k):
-        @pl.when(reach + k > filled)
-        def _():
-            relays(chain2, reach + k, 1)
-
-        sweep(per + k)
 
     def asked(c):
         other = solver(c)
@@ -677,12 +654,56 @@
             def _():
                 question(c, True, me, other).wait_send()
 
-    loop(1, filled + 1, drain3)
+    loop(here + 2, reach, lambda i: relays(chain1, i, 0))
+    def traces0(k):
+        @pl.when(reach + k >= here + 2)
+        def _():
+            relays(chain1, reach + k, 0)
+
+        trace(k)
+
+    loop(0, per, traces0)
+    for fetch in fetches[early:]:
+        fetch.wait()
+    loop(1, reach, lambda i: relays(chain1, i, 1))
+    solve_ring(0)
+    def traces1(k):
+        @pl.when(reach + k >= reach)
+        def _():
+            relays(chain1, reach + k, 1)
+
+        trace(per + k)
+
+    loop(0, per, traces1)
+    fluxes(0)
+    solve_ring(1)
+    loop(1, reach - 2, lambda i: relays(chain2, i, 0))
+    fluxes(1)
+    loop(reach - 2, reach + 1, lambda i: relays(chain2, i, 0))
+    loop(reach + 1, reach + per, lambda i: relays(chain2, i, 0))
+    def drain3(i):
+        relays(chain2, i, 1)
+
+        @pl.when(i <= per)
+        def _():
+            sweep(i - 1)
+
+    loop(1, reach, drain3)
+    loop(max(reach, 1), per + 1, lambda i: sweep(i - 1))
     tip(0)
+    rim(0)
+    rim(1)
     chain1.finish(pieces)
     loop(0, devices, asked)
     loop(1, devices, lambda i: answer(i).wait_send())
-    loop(0, per, drain4)
+    def sweeps1(k):
+        @pl.when(reach + k >= reach)
+        def _():
+            relays(chain2, reach + k, 1)
+
+        sweep(per + k)
+
+    loop(0, per, sweeps1)
     tip(1)
 
     chain2.finish(pieces)
@@ -784,7 +805,9 @@
     wide = np.zeros((total, cols), np.float32)
     wide[:, :1] = extra
     ring = np.stack([inverse, wide]).reshape(2, total, parts, width).transpose(0, 2, 1, 3).copy()
-    tables = [col_table, row_table, row_back, single, ahead, after, mix, mix.T.copy(), ring]
+    mix_back = halves(mix.T.astype(np.float64))
+    mix = halves(mix.astype(np.float64))
+    tables = [col_table, row_table, row_back, single, ahead, after, mix, mix_back, ring]
 
     plane = (problems, rows, cols)
     part = (chunk, rows, cols)

time: 100 us -> 95.5 us (0.955)
  Pallas kernels: 99.1 us -> 94.5 us
    pallas_call x1, Pallas kernels: 77.2 us -> 72.6 us  [local(): pl.pallas_call(functools.partial(solve_kernel, levels=levels, here=here,...]
where the time goes in v5:
time: 95.5 us; the launch traced here: 95.1 us
  Pallas kernels  94.5 us (99%)
    pallas_call x1, Pallas kernels, local(): pl.pallas_call(functools.partial(solve_kernel, levels=levels, here=here,...  72.6 us
    pallas_call x1, Pallas kernels, local(): pl.pallas_call(functools.partial(project_kernel, levels=levels), out_shap...  21.9 us

profile of v5, /device:TPU:0, one launch (start us, length us, event | category | flops | bytes accessed | tf_op | source)
XLA Modules:
  0.0 95.1 jit_solution(14287749154460046105)
XLA Ops:
  0.6 72.6 %solve.1 = (f32[9,16,32,256]{3,2,1,0:T(8,128)}, f32[16,8,256]{2,1,0:T(8,128)}) custom-call(f32[3,8,16,32,256]{4,3,2,1,0:T(8,128)} %mult.1, f32[3,8,16,32,256]{4,3,2,1,0:T(8,128)} %aux_all.1, f32[16,32,256]{2,1,0:T(8,128)} %start_all.1, f32[16,32,256]{2,1,0:T(8,128)} %end_all.1, bf16[2,256,256]{2,1,0:T(8,128)(2,1)} %constant.18.clone.col_all, ...), custom_call_target="tpu_custom_call" | custom-call | tf_op jit(solution)/shard_map/solve/pallas_call | solution.py:826
  73.3 21.9 %project.1 = (f32[3,8,16,32,256]{4,3,2,1,0:T(8,128)}, f32[3,8,16,32,256]{4,3,2,1,0:T(8,128)}) custom-call(f32[9,16,32,256]{3,2,1,0:T(8,128)} %get-tuple-element.4.first.following, f32[9,16,32,256]{3,2,1,0:T(8,128)} %get-tuple-element.4.first.following, f32[16,8,256]{2,1,0:T(8,128)} %get-tuple-element.5.edges, f32[3,8,16,32,256]{4,3,2,1,0:T(8,128)} %mult.1), custom_call_target="tpu_custom_call" | custom-call | tf_op jit(solution)/shard_map/project/pallas_call | solution.py:841

commit v6 on v5

--- a/solution.py
+++ b/solution.py
@@ -675,8 +675,8 @@
         trace(per + k)
 
     loop(0, per, traces1)
+    solve_ring(1)
     fluxes(0)
-    solve_ring(1)
     loop(1, reach - 2, lambda i: relays(chain2, i, 0))
     fluxes(1)
     loop(reach - 2, reach + 1, lambda i: relays(chain2, i, 0))

time: 95.5 us -> 93.7 us (0.981)
  Pallas kernels: 94.5 us -> 92.1 us
    pallas_call x1, Pallas kernels: 72.6 us -> 70.2 us  [local(): pl.pallas_call(functools.partial(solve_kernel, levels=levels, here=here,...]
where the time goes in v6:
time: 93.7 us; the launch traced here: 92.7 us
  Pallas kernels  92.1 us (98%)
    pallas_call x1, Pallas kernels, local(): pl.pallas_call(functools.partial(solve_kernel, levels=levels, here=here,...  70.2 us
    pallas_call x1, Pallas kernels, local(): pl.pallas_call(functools.partial(project_kernel, levels=levels), out_shap...  21.9 us

profile of v6, /device:TPU:0, one launch (start us, length us, event | category | flops | bytes accessed | tf_op | source)
XLA Modules:
  0.0 92.7 jit_solution(3687161181551108075)
XLA Ops:
  0.6 70.2 %solve.1 = (f32[9,16,32,256]{3,2,1,0:T(8,128)}, f32[16,8,256]{2,1,0:T(8,128)}) custom-call(f32[3,8,16,32,256]{4,3,2,1,0:T(8,128)} %mult.1, f32[3,8,16,32,256]{4,3,2,1,0:T(8,128)} %aux_all.1, f32[16,32,256]{2,1,0:T(8,128)} %start_all.1, f32[16,32,256]{2,1,0:T(8,128)} %end_all.1, bf16[2,256,256]{2,1,0:T(8,128)(2,1)} %constant.18.clone.col_all, ...), custom_call_target="tpu_custom_call" | custom-call | tf_op jit(solution)/shard_map/solve/pallas_call | solution.py:826
  70.9 21.9 %project.1 = (f32[3,8,16,32,256]{4,3,2,1,0:T(8,128)}, f32[3,8,16,32,256]{4,3,2,1,0:T(8,128)}) custom-call(f32[9,16,32,256]{3,2,1,0:T(8,128)} %get-tuple-element.4.first.following, f32[9,16,32,256]{3,2,1,0:T(8,128)} %get-tuple-element.4.first.following, f32[16,8,256]{2,1,0:T(8,128)} %get-tuple-element.5.edges, f32[3,8,16,32,256]{4,3,2,1,0:T(8,128)} %mult.1), custom_call_target="tpu_custom_call" | custom-call | tf_op jit(solution)/shard_map/project/pallas_call | solution.py:841

commit v7 on v6

--- a/solution.py
+++ b/solution.py
@@ -761,7 +761,7 @@
         next_mult[2, 0, b] = mult_second + PENALTY * (grad_second - out_beside)
         return carry
 
-    lax.fori_loop(0, problems, one, 0, unroll=4)
+    lax.fori_loop(0, problems, one, 0, unroll=16)
 
 
 def params(which=None):

time: 93.7 us -> 92.3 us (0.985)
  Pallas kernels: 92.1 us -> 90.8 us
    pallas_call x1, Pallas kernels: 21.9 us -> 20.6 us  [local(): pl.pallas_call(functools.partial(project_kernel, levels=levels), out_shap...]
where the time goes in v7:
time: 92.3 us; the launch traced here: 91.4 us
  Pallas kernels  90.8 us (98%)
    pallas_call x1, Pallas kernels, local(): pl.pallas_call(functools.partial(solve_kernel, levels=levels, here=here,...  70.2 us
    pallas_call x1, Pallas kernels, local(): pl.pallas_call(functools.partial(project_kernel, levels=levels), out_shap...  20.6 us

profile of v7, /device:TPU:0, one launch (start us, length us, event | category | flops | bytes accessed | tf_op | source)
XLA Modules:
  0.0 91.4 jit_solution(2481308841118059019)
XLA Ops:
  0.6 70.2 %solve.1 = (f32[9,16,32,256]{3,2,1,0:T(8,128)}, f32[16,8,256]{2,1,0:T(8,128)}) custom-call(f32[3,8,16,32,256]{4,3,2,1,0:T(8,128)} %mult.1, f32[3,8,16,32,256]{4,3,2,1,0:T(8,128)} %aux_all.1, f32[16,32,256]{2,1,0:T(8,128)} %start_all.1, f32[16,32,256]{2,1,0:T(8,128)} %end_all.1, bf16[2,256,256]{2,1,0:T(8,128)(2,1)} %constant.18.clone.col_all, ...), custom_call_target="tpu_custom_call" | custom-call | tf_op jit(solution)/shard_map/solve/pallas_call | solution.py:826
  70.9 20.6 %project.1 = (f32[3,8,16,32,256]{4,3,2,1,0:T(8,128)}, f32[3,8,16,32,256]{4,3,2,1,0:T(8,128)}) custom-call(f32[9,16,32,256]{3,2,1,0:T(8,128)} %get-tuple-element.4.first.following, f32[9,16,32,256]{3,2,1,0:T(8,128)} %get-tuple-element.4.first.following, f32[16,8,256]{2,1,0:T(8,128)} %get-tuple-element.5.edges, f32[3,8,16,32,256]{4,3,2,1,0:T(8,128)} %mult.1), custom_call_target="tpu_custom_call" | custom-call | tf_op jit(solution)/shard_map/project/pallas_call | solution.py:841
